TPU v7x, 32 devices: a whole 2x2x4 slice. The times are simulated.
32 devices in a mesh: fsdp: 4 (over x, core), ctx: 2 (over y), tp: 4 (over z).
Axes of the slice: x: 2, y: 2, z: 4, core: 2. Of those that a mesh axis runs over, the one named last changes fastest.
Arguments:
- tokens: bfloat16 [8, 1024, 2048], P('fsdp', 'ctx'), may hold values from -6 to 6
- attn_gain: bfloat16 [2048], P('fsdp'), may hold values from 0.5 to 1.5
- w_query: bfloat16 [2048, 1024], P('fsdp', 'tp'), may hold values from -0.125 to 0.125
- key_matrix: bfloat16 [2048, 256], P('fsdp', 'tp'), may hold values from -0.125 to 0.125
- value_matrix: bfloat16 [2048, 256], P('fsdp', 'tp'), may hold values from -0.125 to 0.125
- query_gain: bfloat16 [64], P('fsdp'), may hold values from 0.5 to 1.5
- key_gain: bfloat16 [64], P('fsdp'), may hold values from 0.5 to 1.5
- w_out: bfloat16 [1024, 2048], P('tp', 'fsdp'), may hold values from -6 to 6
- ffn_gain: bfloat16 [2048], P('fsdp'), may hold values from 0.5 to 1.5
- w_gate: bfloat16 [2048, 1024], P('fsdp', 'tp'), may hold values from -0.125 to 0.125
- w_up: bfloat16 [2048, 1024], P('fsdp', 'tp'), may hold values from -0.125 to 0.125
- w_down: bfloat16 [1024, 2048], P('tp', 'fsdp'), may hold values from -0.1875 to 0.1875
- prefix_len: int32 [8], P('fsdp'), may hold values from 102 to 512
- out_grad: bfloat16 [8, 1024, 2048], P('fsdp', 'ctx'), may hold values from -6 to 6
Outputs:
- layer_out: bfloat16 [8, 1024, 2048], P('fsdp', 'ctx')
- input_grad: bfloat16 [8, 1024, 2048], P('fsdp', 'ctx')
- grad_attn_gain: float32 [2048], P('fsdp')
- grad_query: float32 [2048, 1024], P('fsdp', 'tp')
- grad_key: float32 [2048, 256], P('fsdp', 'tp')
- grad_value: float32 [2048, 256], P('fsdp', 'tp')
- grad_query_gain: float32 [64], P('fsdp')
- grad_key_gain: float32 [64], P('fsdp')
- grad_out: float32 [1024, 2048], P('tp', 'fsdp')
- grad_ffn_gain: float32 [2048], P('fsdp')
- grad_gate: float32 [2048, 1024], P('fsdp', 'tp')
- grad_up: float32 [2048, 1024], P('fsdp', 'tp')
- grad_down: float32 [1024, 2048], P('tp', 'fsdp')
All inputs are finite; a program needn't handle non-finite values.
Results may differ from a plain program's by a relative error of at most 0.025.
Values may be sent and summed in bfloat16 or wider, within the bound.
No kernel may reach another device: no remote copies, remote signals or barrier semaphores. Data moves between devices by JAX's collectives and lax.ppermute only.
A program may use at most 192 MiB of HBM per device.

v0:
```python
import functools

import jax
import jax.numpy as jnp
from jax import lax
from jax.sharding import PartitionSpec as P

EPSILON = 1e-06
NEGATIVE = -1e30
ROPE_BASE = 10000.0


def rms_norm(values, gain):
    return values * lax.rsqrt(jnp.mean(values * values, axis=-1, keepdims=True) + EPSILON) * gain


def rotate(values, cos_table, sin_table):
    half_dim = values.shape[-1] // 2
    turned = jnp.concatenate([-values[..., half_dim:], values[..., :half_dim]], axis=-1)
    return values * cos_table + turned * sin_table


def rotary_tables(positions, head_dim):
    inverse_freq = ROPE_BASE ** (-jnp.arange(0, head_dim, 2).astype(jnp.float32) / head_dim)
    angles = positions.astype(jnp.float32)[:, None] * inverse_freq[None, :]
    cos_half = jnp.cos(angles)
    sin_half = jnp.sin(angles)
    return (jnp.concatenate([cos_half, cos_half], -1), jnp.concatenate([sin_half, sin_half], -1))


def query_key_post(
    query_raw, unnormed_key, query_gain, key_gain, cos_table, sin_table, seq_count, block_len
):
    head_dim = query_gain.shape[0]
    query_heads = query_raw.reshape(seq_count, block_len, -1, head_dim)
    key_heads = unnormed_key.reshape(seq_count, block_len, -1, head_dim)
    cos_wide = cos_table[None, :, None, :]
    sin_wide = sin_table[None, :, None, :]
    return (
        rotate(rms_norm(query_heads, query_gain), cos_wide, sin_wide),
        rotate(rms_norm(key_heads, key_gain), cos_wide, sin_wide),
    )


def swiglu(gate_proj, up_proj):
    return jax.nn.silu(gate_proj) * up_proj


def outer_sum(left, right):
    return lax.dot_general(
        left, right, (((0,), (0,)), ((), ())), preferred_element_type=jnp.float32
    )


def times_transposed(left, right):
    return lax.dot_general(
        left, right, (((1,), (1,)), ((), ())), preferred_element_type=jnp.float32
    )


def pack_grads(gradients, grad_dims, pieces):
    columns = [
        jnp.moveaxis(gradient, dim_index, 0).reshape(pieces, -1)
        for gradient, dim_index in zip(gradients, grad_dims)
    ]
    return jnp.concatenate(columns, axis=1)


def unpack_grads(packed, gradients, grad_dims, pieces):
    results = []
    offset = 0
    for gradient, dim_index in zip(gradients, grad_dims):
        moved_shape = jnp.moveaxis(gradient, dim_index, 0).shape
        width = gradient.size // pieces
        segment = packed[:, offset : offset + width]
        offset = offset + width
        shaped = segment.reshape((-1,) + tuple(moved_shape[1:]))
        results.append(jnp.moveaxis(shaped, 0, dim_index))
    return results


def shards(
    tokens,
    attn_gain,
    w_query,
    key_matrix,
    value_matrix,
    query_gain,
    key_gain,
    w_out,
    ffn_gain,
    w_gate,
    w_up,
    w_down,
    prefix_len,
    out_grad,
):
    (
        full_attn_gain,
        full_query,
        full_key,
        full_value,
        full_query_gain,
        full_key_gain,
        full_out,
        full_ffn_gain,
        full_gate,
        full_up,
        full_down,
    ) = (
        lax.all_gather(attn_gain, "fsdp", axis=0, tiled=True),
        lax.all_gather(w_query, "fsdp", axis=0, tiled=True),
        lax.all_gather(key_matrix, "fsdp", axis=0, tiled=True),
        lax.all_gather(value_matrix, "fsdp", axis=0, tiled=True),
        lax.all_gather(query_gain, "fsdp", axis=0, tiled=True),
        lax.all_gather(key_gain, "fsdp", axis=0, tiled=True),
        lax.all_gather(w_out, "fsdp", axis=1, tiled=True),
        lax.all_gather(ffn_gain, "fsdp", axis=0, tiled=True),
        lax.all_gather(w_gate, "fsdp", axis=0, tiled=True),
        lax.all_gather(w_up, "fsdp", axis=0, tiled=True),
        lax.all_gather(w_down, "fsdp", axis=1, tiled=True),
    )
    seq_count, block_len, model_dim = tokens.shape
    token_rows = seq_count * block_len
    head_dim = full_query_gain.shape[0]
    head_count = full_query.shape[1] // head_dim
    kv_count = full_key.shape[1] // head_dim
    group_size = head_count // kv_count
    ctx_count = lax.axis_size("ctx")
    ctx_index = lax.axis_index("ctx")
    fsdp_count = lax.axis_size("fsdp")
    seq_len = block_len * ctx_count
    scale_factor = head_dim ** (-0.5)
    tp_count = lax.axis_size("tp")
    share_rows = token_rows // tp_count
    share_start = lax.axis_index("tp") * share_rows

    def own_rows(values):
        return lax.dynamic_slice_in_dim(values, share_start, share_rows, 0)

    query_pos = ctx_index * block_len + jnp.arange(block_len, dtype=jnp.int32)
    cos_table, sin_table = rotary_tables(query_pos, head_dim)
    attn_gain32 = full_attn_gain.astype(jnp.float32)
    ffn_gain32 = full_ffn_gain.astype(jnp.float32)
    query_gain32 = full_query_gain.astype(jnp.float32)
    key_gain32 = full_key_gain.astype(jnp.float32)
    inputs = tokens.astype(jnp.float32).reshape(token_rows, model_dim)
    normalized_input = rms_norm(inputs, attn_gain32).astype(jnp.bfloat16)
    query_raw = jnp.dot(normalized_input, full_query, preferred_element_type=jnp.float32)
    unnormed_key = jnp.dot(normalized_input, full_key, preferred_element_type=jnp.float32)
    value_reduced = jnp.dot(
        normalized_input, full_value, preferred_element_type=jnp.float32
    ).astype(jnp.bfloat16)
    post_fn = functools.partial(
        query_key_post,
        cos_table=cos_table,
        sin_table=sin_table,
        seq_count=seq_count,
        block_len=block_len,
    )
    (rotated_query, key_rot), post_pull = jax.vjp(
        post_fn, query_raw, unnormed_key, query_gain32, key_gain32
    )
    query_grp = rotated_query.astype(jnp.bfloat16).reshape(
        seq_count, block_len, kv_count, group_size, head_dim
    )
    key_low = key_rot.astype(jnp.bfloat16)
    value_heads = value_reduced.reshape(seq_count, block_len, kv_count, head_dim)
    keys_all, values_all = (
        lax.all_gather(key_low, "ctx", axis=1, tiled=True),
        lax.all_gather(value_heads, "ctx", axis=1, tiled=True),
    )
    key_blocks = jnp.moveaxis(
        keys_all.reshape(seq_count, ctx_count, block_len, kv_count, head_dim), 1, 0
    )
    value_blocks = jnp.moveaxis(
        values_all.reshape(seq_count, ctx_count, block_len, kv_count, head_dim), 1, 0
    )
    block_ids = jnp.arange(ctx_count, dtype=jnp.int32)

    def score_block(key_blk, block_id):
        raw_scores = (
            jnp.einsum("sqkgd,sjkd->skgqj", query_grp, key_blk, preferred_element_type=jnp.float32)
            * scale_factor
        )
        key_pos = block_id * block_len + jnp.arange(block_len, dtype=jnp.int32)
        causal = key_pos[None, :] <= query_pos[:, None]
        opened = key_pos[None, None, :] < prefix_len[:, None, None]
        allowed = causal[None] | opened
        return jnp.where(allowed[:, None, None], raw_scores, NEGATIVE)

    def max_step(run_state, scan_item):
        key_blk, block_id = scan_item
        run_max, run_sum = run_state
        scores = score_block(key_blk, block_id)
        new_max = jnp.maximum(run_max, jnp.max(scores, axis=-1))
        new_sum = run_sum * jnp.exp(run_max - new_max) + jnp.sum(
            jnp.exp(scores - new_max[..., None]), axis=-1
        )
        new_state = (new_max, new_sum)
        return (new_state, None)

    stat_shape = (seq_count, kv_count, group_size, block_len)
    (run_max, run_sum), _ = lax.scan(
        max_step,
        (jnp.full(stat_shape, NEGATIVE, jnp.float32), jnp.zeros(stat_shape, jnp.float32)),
        (key_blocks, block_ids),
    )
    log_total = run_max + jnp.log(run_sum)

    def out_step(running, scan_item):
        key_blk, value_blk, block_id = scan_item
        prob_vals = jnp.exp(score_block(key_blk, block_id) - log_total[..., None])
        new_running = running + jnp.einsum(
            "skgqj,sjkd->sqkgd",
            prob_vals.astype(jnp.bfloat16),
            value_blk,
            preferred_element_type=jnp.float32,
        )
        return (new_running, None)

    out_shape = (seq_count, block_len, kv_count, group_size, head_dim)
    attended, _ = lax.scan(
        out_step, jnp.zeros(out_shape, jnp.float32), (key_blocks, value_blocks, block_ids)
    )
    attended_low = attended.reshape(token_rows, head_count * head_dim).astype(jnp.bfloat16)
    attn_part = jnp.dot(attended_low, full_out, preferred_element_type=jnp.float32)
    residual = inputs + lax.psum(attn_part.astype(jnp.bfloat16), "tp").astype(jnp.float32)
    residual_own = own_rows(residual)
    ffn_in = rms_norm(residual, ffn_gain32).astype(jnp.bfloat16)
    gate_proj = jnp.dot(ffn_in, full_gate, preferred_element_type=jnp.float32)
    up_proj = jnp.dot(ffn_in, full_up, preferred_element_type=jnp.float32)
    hidden_f, swiglu_pull = jax.vjp(swiglu, gate_proj, up_proj)
    hidden = hidden_f.astype(jnp.bfloat16)
    ffn_part = jnp.dot(hidden, full_down, preferred_element_type=jnp.float32)
    layer_low = (
        residual + lax.psum(ffn_part.astype(jnp.bfloat16), "tp").astype(jnp.float32)
    ).astype(jnp.bfloat16)
    grad_low = out_grad.reshape(token_rows, model_dim)
    grad_down = outer_sum(hidden, grad_low)
    dhidden = times_transposed(grad_low, full_down)
    dgate_f, dup_f = swiglu_pull(dhidden)
    dgate = dgate_f.astype(jnp.bfloat16)
    dup = dup_f.astype(jnp.bfloat16)
    grad_gate = outer_sum(ffn_in, dgate)
    grad_up = outer_sum(ffn_in, dup)
    dffn_part = times_transposed(dgate, full_gate) + times_transposed(dup, full_up)
    dffn_in = lax.psum(dffn_part.astype(jnp.bfloat16), "tp").astype(jnp.float32)
    _, ffn_norm_pull = jax.vjp(rms_norm, residual, ffn_gain32)
    dres_norm, _ = ffn_norm_pull(dffn_in)
    dresidual = grad_low.astype(jnp.float32) + dres_norm
    _, own_pull = jax.vjp(rms_norm, residual_own, ffn_gain32)
    _, grad_ffn_gain = own_pull(own_rows(dffn_in))
    dres_low = dresidual.astype(jnp.bfloat16)
    grad_out = outer_sum(attended_low, dres_low)
    dattended = times_transposed(dres_low, full_out).astype(jnp.bfloat16)
    dout_grp = dattended.reshape(out_shape)
    delta = jnp.transpose(jnp.sum(dout_grp.astype(jnp.float32) * attended, axis=-1), (0, 2, 3, 1))

    def back_step(running, scan_item):
        key_blk, value_blk, block_id = scan_item
        prob_vals = jnp.exp(score_block(key_blk, block_id) - log_total[..., None])
        prob_low = prob_vals.astype(jnp.bfloat16)
        value_grad = jnp.einsum(
            "skgqj,sqkgd->sjkd", prob_low, dout_grp, preferred_element_type=jnp.float32
        )
        dprob = jnp.einsum(
            "sqkgd,sjkd->skgqj", dout_grp, value_blk, preferred_element_type=jnp.float32
        )
        dscore = (prob_vals * (dprob - delta[..., None])).astype(jnp.bfloat16)
        new_running = (
            running
            + jnp.einsum("skgqj,sjkd->sqkgd", dscore, key_blk, preferred_element_type=jnp.float32)
            * scale_factor
        )
        key_grad = (
            jnp.einsum("skgqj,sqkgd->sjkd", dscore, query_grp, preferred_element_type=jnp.float32)
            * scale_factor
        )
        return (new_running, (key_grad, value_grad))

    dquery_rot, (key_grads, value_grads) = lax.scan(
        back_step, jnp.zeros(out_shape, jnp.float32), (key_blocks, value_blocks, block_ids)
    )
    key_grads = jnp.moveaxis(key_grads, 0, 1).reshape(seq_count, seq_len, kv_count, head_dim)
    value_grads = jnp.moveaxis(value_grads, 0, 1).reshape(seq_count, seq_len, kv_count, head_dim)
    stacked_grads = jnp.stack((key_grads, value_grads), axis=0)
    owned_grads = lax.psum_scatter(
        stacked_grads.astype(jnp.bfloat16), "ctx", scatter_dimension=2, tiled=True
    ).astype(jnp.float32)
    dkey_rot = owned_grads[0]
    dvalue = owned_grads[1]
    dquery_raw, dkey_raw, grad_query_gain, grad_key_gain = post_pull(
        (dquery_rot.reshape(seq_count, block_len, head_count, head_dim), dkey_rot)
    )
    dq_low = dquery_raw.astype(jnp.bfloat16)
    dk_low = dkey_raw.astype(jnp.bfloat16)
    dv_low = dvalue.reshape(token_rows, kv_count * head_dim).astype(jnp.bfloat16)
    grad_query = outer_sum(normalized_input, dq_low)
    grad_key = outer_sum(normalized_input, dk_low)
    grad_value = outer_sum(normalized_input, dv_low)
    dnormed_part = (
        times_transposed(dq_low, full_query)
        + times_transposed(dk_low, full_key)
        + times_transposed(dv_low, full_value)
    )
    dnormed, grad_query_gain, grad_key_gain, grad_ffn_gain = (
        lax.psum(dnormed_part.astype(jnp.bfloat16), "tp").astype(jnp.float32),
        lax.psum(grad_query_gain.astype(jnp.bfloat16), "tp").astype(jnp.float32),
        lax.psum(grad_key_gain.astype(jnp.bfloat16), "tp").astype(jnp.float32),
        lax.psum(grad_ffn_gain.astype(jnp.bfloat16), "tp").astype(jnp.float32),
    )
    _, attn_norm_pull = jax.vjp(rms_norm, inputs, attn_gain32)
    dinput_norm, grad_attn_gain = attn_norm_pull(dnormed)
    input_grad = (dresidual + dinput_norm).astype(jnp.bfloat16)
    gradients = (
        grad_attn_gain,
        grad_query,
        grad_key,
        grad_value,
        grad_query_gain,
        grad_key_gain,
        grad_out,
        grad_ffn_gain,
        grad_gate,
        grad_up,
        grad_down,
    )
    grad_dims = (0, 0, 0, 0, 0, 0, 1, 0, 0, 0, 1)
    piece_count = fsdp_count * ctx_count
    packed = pack_grads(gradients, grad_dims, piece_count)
    reduced = lax.psum_scatter(
        packed.astype(jnp.bfloat16), ("fsdp", "ctx"), scatter_dimension=0, tiled=True
    ).astype(jnp.float32)
    collected_rows = lax.all_gather(reduced.astype(jnp.bfloat16), "ctx", axis=0, tiled=True).astype(
        reduced.dtype
    )
    collected = unpack_grads(collected_rows, gradients, grad_dims, piece_count)
    return (
        layer_low.reshape(seq_count, block_len, model_dim),
        input_grad.reshape(seq_count, block_len, model_dim),
        collected[0],
        collected[1],
        collected[2],
        collected[3],
        collected[4],
        collected[5],
        collected[6],
        collected[7],
        collected[8],
        collected[9],
        collected[10],
    )


def solution(mesh):
    placed = (
        P("fsdp", "ctx", None),
        P("fsdp"),
        P("fsdp", "tp"),
        P("fsdp", "tp"),
        P("fsdp", "tp"),
        P("fsdp"),
        P("fsdp"),
        P("tp", "fsdp"),
        P("fsdp"),
        P("fsdp", "tp"),
        P("fsdp", "tp"),
        P("tp", "fsdp"),
        P("fsdp"),
        P("fsdp", "ctx", None),
    )
    return jax.shard_map(
        shards,
        mesh=mesh,
        in_specs=placed,
        out_specs=(
            P("fsdp", "ctx", None),
            P("fsdp", "ctx", None),
            P("fsdp"),
            P("fsdp", "tp"),
            P("fsdp", "tp"),
            P("fsdp", "tp"),
            P("fsdp"),
            P("fsdp"),
            P("tp", "fsdp"),
            P("fsdp"),
            P("fsdp", "tp"),
            P("fsdp", "tp"),
            P("tp", "fsdp"),
        ),
        check_vma=False,
    )
```

profile of v0, /device:TPU:0, one launch (start us, length us, event | category | flops | bytes accessed | tf_op | source)
XLA Modules:
  0.0 1090.6 jit_solution(5404489563238779598)
XLA Ops:
  12.7 6.2 all-gather
  18.9 8.2 all_gather.45
  34.2 7.3 all-reduce.9
  60.8 6.6 all_gather.44
  75.3 22.4 %while.39 = (s32[]{:T(128)}, f32[2,1,4,512]{3,2,0,1:T(4,128)S(1)}, f32[2,1,4,512]{3,2,0,1:T(4,128)S(1)}, s32[2]{0:T(128)S(1)}, s32[2]{0:T(128)S(1)}, /*index=5*/...) while((s32[]{:T(128)}, f32[2,1,4,512]{3,2,0,1:T(4,128)S(1)}, ...), condition=%wide.region_6.7_spmd.clone, body=%wide.region_3.6_spmd.clone.sunk | while | flops 283924480 | bytes 19755172 | solution.py:204
  98.4 11.8 %while.40 = (s32[]{:T(128)}, f32[2,512,1,4,64]{1,4,3,0,2:T(8,128)S(1)}, bf16[2,2,512,1,64]{2,4,1,3,0:T(8,128)(2,1)}, s32[2]{0:T(128)S(1)}, s32[2]{0:T(128)S(1)},...) while((s32[]{:T(128)}, ...), condition=%wide.region_8.9_spmd.clone, body=%wide.region_7.8_spmd.clone.sunk | while | flops 546572288 | bytes 4486311 | solution.py:223
  122.9 148.2 %all-reduce.15.cloned.1.call-done = bf16[1024,2048]{1,0:T(8,128)(2,1)} async-done(((bf16[1024,2048]{1,0:T(8,128)(2,1)}), bf16[1024,2048]{1,0:T(8,128)(2,1)}) %all-reduce.15.cloned.1.call-update) | async-done | bytes 4194320 | tf_op jit(solution)/shard_map/psum | solution.py:228
  293.0 13.3 %all-gather.16.cloned.1.call-done = bf16[2048,256]{1,0:T(8,128)(2,1)} async-done(((bf16[512,256]{1,0:T(8,128)(2,1)}), bf16[2048,256]{1,0:T(8,128)(2,1)}) %all-gather.16.cloned.1.call-update) | async-done | bytes 1048592 | tf_op jit(solution)/shard_map/all_gather | solution.py:120
  311.1 13.4 %all-gather.18.cloned.1.call-done = bf16[256,2048]{1,0:T(8,128)(2,1)} async-done(((bf16[256,512]{1,0:T(8,128)(2,1)}), bf16[256,2048]{1,0:T(8,128)(2,1)}) %all-gather.18.cloned.1.call-update) | async-done | bytes 1048592 | tf_op jit(solution)/shard_map/all_gather | solution.py:121
  338.9 150.7 %all-reduce.17.cloned.1.call-done = bf16[1024,2048]{1,0:T(8,128)(2,1)} async-done(((bf16[1024,2048]{1,0:T(8,128)(2,1)}), bf16[1024,2048]{1,0:T(8,128)(2,1)}) %all-reduce.17.cloned.1.call-update) | async-done | bytes 4194320 | tf_op jit(solution)/shard_map/psum | solution.py:248
  489.6 6.8 multiply_reduce_fusion
  496.7 7.5 fusion.80
  512.8 45.9 %while.41 = (s32[]{:T(128)}, f32[2,512,1,4,64]{1,4,3,0,2:T(8,128)S(1)}, bf16[2,2,512,1,64]{2,4,1,3,0:T(8,128)(2,1)}, bf16[2,2,512,1,64]{2,4,1,3,0:T(8,128)(2,1)}...) while((s32[]{:T(128)}, ...), condition=%wide.region_16.17_spmd.clone, body=%wide.region_15.16_spmd.clone.sunk | while | flops 1364789248 | bytes 100594080 | solution.py:282
  566.5 10.8 reduce-scatter.2.cloned.1.call-done
  630.0 13.4 %all-reduce.7 = (bf16[8,8]{1,0:T(8,128)(2,1)S(1)}, bf16[8,8]{1,0:T(8,128)(2,1)S(1)}, bf16[8,256]{1,0:T(8,128)(2,1)S(1)}) all-reduce(bf16[8,8]{1,0:T(8,128)(2,1)S(1)} %reshape.780, bf16[8,8]{1,0:T(8,128)(2,1)S(1)} %reshape.781, bf16[8,256]{1,0:T(8,128)(2,1)S(1)} %reshape.783), channel_id=1, replica_groups=mesh['fsdp'=4,'ctx'=2,'tp'=4] {'tp'}, use_global_device_ids=true, to_apply=%region_24.25 | all-reduce | flops 2176 | bytes 8704 | tf_op jit(solution)/shard_map/psum | solution.py:309
  643.4 233.6 %all-reduce.21.cloned.1.call-done = (bf16[1024,2048]{1,0:T(8,128)(2,1)}, bf16[1024,2048]{1,0:T(8,128)(2,1)}) async-done(((bf16[1024,2048]{1,0:T(8,128)(2,1)}, bf16[1024,2048]{1,0:T(8,128)(2,1)}), (bf16[1024,2048]{1,0:T(8,128)(2,1)}, bf16[1024,2048]{1,0:T(8,128)(2,1)})) %all-reduce.21.cloned.1.call-update) | async-done | bytes 8388624 | tf_op jit(solution)/shard_map/psum | solution.py:237
  890.1 7.1 dynamic-update-slice.8
  898.6 6.8 dynamic-update-slice.10
  905.4 6.8 dynamic-update-slice.11
  912.2 6.7 dynamic-update-slice.12
  919.6 97.4 %all-reduce.19.cloned.1.call-done = bf16[8,360976]{1,0:T(8,128)(2,1)} async-done(((bf16[8,360976]{1,0:T(8,128)(2,1)}), bf16[8,360976]{1,0:T(8,128)(2,1)}) %all-reduce.19.cloned.1.call-update) | async-done | bytes 5775632
  1017.0 6.2 dynamic-slice_bitcast_fusion
  1023.2 14.9 %fusion.82 = (bf16[1024,2048]{1,0:T(8,128)(2,1)}, bf16[1024,2048]{1,0:T(8,128)(2,1)}) fusion(f32[1024,2048]{1,0:T(8,128)} %copy-done.4, bf16[1024,2048]{1,0:T(8,128)(2,1)} %get-tuple-element.498, bf16[2,512,2048]{2,1,0:T(8,128)(2,1)} %param.20, f32[1024]{0:T(1024)S(1)} %multiply_multiply_fusion.3, f32[2048]{0:T(1024)S(1)} %bitcast.468, ...), kind=kLoop, calls=%fused_computation.93 | loop fusion | flops 29360128 | bytes 33570816 | tf_op jit(solution)/shard_map/convert_element_type | solution.py:315
  1038.1 27.2 %all-gather.20.cloned.1.call-done = bf16[2,1,360976]{2,1,0:T(2,128)(2,1)} async-done(((bf16[1,1,360976]{2,1,0:T(2,128)(2,1)}), bf16[2,1,360976]{2,1,0:T(2,128)(2,1)}) %all-gather.20.cloned.1.call-update) | async-done | bytes 1443920 | tf_op jit(solution)/shard_map/all_gather | solution.py:335
  (378 shorter events, 270.8 us)
Async XLA Ops:
  7.2 61.1 %all-gather.10.cloned.1.call-start = ((), (), s32[]{:S(2)}) async-start(), calls=%async_computation.1 | async-start | bytes 1310720 | tf_op jit(solution)/shard_map/all_gather | solution.py:112
  7.9 103.0 %all-gather.12.cloned.1.call-start = ((), (), s32[]{:S(2)}) async-start(), calls=%async_computation.2 | async-start | bytes 1310720 | tf_op jit(solution)/shard_map/all_gather | solution.py:117
  8.7 262.5 %all-reduce.15.cloned.1.call-start = ((), (), s32[]{:S(2)}) async-start(), calls=%async_computation.3 | async-start | bytes 8388608 | tf_op jit(solution)/shard_map/psum | solution.py:228
  12.0 19.6 %copy-start.51 = (f32[1,4,2,128]{3,1,2,0:T(4,128)}, f32[1,4,2,128]{3,1,2,0:T(4,128)S(1)}, u32[]{:S(2)}) copy-start(f32[1,4,2,128]{3,1,2,0:T(4,128)S(1)} %copy.136) | copy-start | bytes 12292
  18.9 29.2 %copy-start.41 = (f32[4,1,512]{2,1,0:T(1,128)}, f32[4,1,512]{2,1,0:T(1,128)S(1)}, u32[]{:S(2)}) copy-start(f32[4,1,512]{2,1,0:T(1,128)S(1)} %convert_element_type.229) | copy-start | bytes 24580
  32.2 21.2 %copy-start.44 = (f32[2,512]{1,0:T(2,128)}, f32[2,512]{1,0:T(2,128)S(1)}, u32[]{:S(2)}) copy-start(f32[2,512]{1,0:T(2,128)S(1)} %rsqrt.55) | copy-start | bytes 12292
  32.5 21.0 %copy-start.12 = (f32[2,512,1,64]{1,0,3,2:T(2,128)}, f32[2,512,1,64]{1,0,3,2:T(2,128)S(1)}, u32[]{:S(2)}) copy-start(f32[2,512,1,64]{1,0,3,2:T(2,128)S(1)} %reshape.768) | copy-start | bytes 786436
  42.0 32.7 %copy-start.19 = (f32[512,64]{0,1:T(8,128)}, f32[512,64]{0,1:T(8,128)S(1)}, u32[]{:S(2)}) copy-start(f32[512,64]{0,1:T(8,128)S(1)} %get-tuple-element.546) | copy-start | bytes 393220
  42.1 32.7 %copy-start.21 = (f32[512,64]{0,1:T(8,128)}, f32[512,64]{0,1:T(8,128)S(1)}, u32[]{:S(2)}) copy-start(f32[512,64]{0,1:T(8,128)S(1)} %get-tuple-element.545) | copy-start | bytes 393220
  53.5 21.3 %copy-start.57 = (f32[64]{0:T(128)}, f32[64]{0:T(128)S(1)}, u32[]{:S(2)}) copy-start(f32[64]{0:T(128)S(1)} %convert_element_type.194) | copy-start | bytes 772
  115.6 172.6 %all-gather.14.cloned.1.call-start = ((), (), s32[]{:S(2)}) async-start(), calls=%async_computation.4 | async-start | bytes 1310720 | tf_op jit(solution)/shard_map/all_gather | solution.py:119
  116.2 190.1 %all-gather.16.cloned.1.call-start = ((), (), s32[]{:S(2)}) async-start(), calls=%async_computation.5 | async-start | bytes 1310720 | tf_op jit(solution)/shard_map/all_gather | solution.py:120
  116.8 207.7 %all-gather.18.cloned.1.call-start = ((), (), s32[]{:S(2)}) async-start(), calls=%async_computation.6 | async-start | bytes 1310720 | tf_op jit(solution)/shard_map/all_gather | solution.py:121
  117.4 372.2 %all-reduce.17.cloned.1.call-start = ((), (), s32[]{:S(2)}) async-start(), calls=%async_computation.7 | async-start | bytes 8388608 | tf_op jit(solution)/shard_map/psum | solution.py:248
  334.4 242.9 %reduce-scatter.2.cloned.1.call-start = ((), (), s32[]{:S(2)}) async-start(), calls=%async_computation.8 | async-start | bytes 786432 | tf_op jit(solution)/shard_map/reduce_scatter | solution.py:288
  512.8 45.9 %copy-start.20 = (f32[512,64]{0,1:T(8,128)S(1)}, f32[512,64]{0,1:T(8,128)}, u32[]{:S(2)}) copy-start(f32[512,64]{0,1:T(8,128)} %copy-done.19) | copy-start | bytes 393220
  563.5 313.5 %all-reduce.21.cloned.1.call-start = ((), (), s32[]{:S(2)}) async-start(), calls=%async_computation.11 | async-start | bytes 16777216 | tf_op jit(solution)/shard_map/psum | solution.py:237
  585.6 431.4 %all-reduce.19.cloned.1.call-start = ((), (), s32[]{:S(2)}) async-start(), calls=%async_computation.10 | async-start | bytes 11554816
  622.4 254.6 %copy-start.42 = (f32[4,1,512]{2,1,0:T(1,128)S(1)}, f32[4,1,512]{2,1,0:T(1,128)}, u32[]{:S(2)}) copy-start(f32[4,1,512]{2,1,0:T(1,128)} %copy-done.41) | copy-start | bytes 24580
  622.4 254.6 %copy-start.50 = (f32[1024]{0:T(1024)S(1)}, f32[1024]{0:T(1024)}, u32[]{:S(2)}) copy-start(f32[1024]{0:T(1024)} %copy-done.49) | copy-start | bytes 12292
  883.0 22.5 %copy-start.17 = (bf16[8,65536]{1,0:T(8,128)(2,1)S(1)}, bf16[8,65536]{1,0:T(8,128)(2,1)}, u32[]{:S(2)}) copy-start(bf16[8,65536]{1,0:T(8,128)(2,1)} %reshape.785) | copy-start | bytes 3145732
  898.6 20.4 %copy-start.63 = (u32[32]{0:T(128)S(1)}, u32[32]{0:T(128)}, u32[]{:S(2)}) copy-start(u32[32]{0:T(128)} %constant.133) | copy-start | bytes 388
  912.2 111.0 %copy-start.52 = (f32[1,4,2,128]{3,1,2,0:T(4,128)S(1)}, f32[1,4,2,128]{3,1,2,0:T(4,128)}, u32[]{:S(2)}) copy-start(f32[1,4,2,128]{3,1,2,0:T(4,128)} %copy-done.51) | copy-start | bytes 12292
  919.0 146.4 %all-gather.20.cloned.1.call-start = ((), (), s32[]{:S(2)}) async-start(), calls=%async_computation.9 | async-start | bytes 4333056 | tf_op jit(solution)/shard_map/all_gather | solution.py:335
  (60 other events, 361.4 us)
Sparse Core Ops, SparseCore 0:
  9.5 20.8 all-gather.9
  32.0 16.6 all-gather.11
  115.8 155.3 all-reduce.14
  272.5 15.6 all-gather.13
  289.6 16.6 all-gather.15
  307.8 16.6 all-gather.17
  334.6 154.9 all-reduce.16
  563.7 13.5 reduce-scatter.1
  585.7 291.3 all-reduce.20
  919.1 97.8 all-reduce.18
  1023.3 41.9 all-gather.19
where the time goes:
time: 1100 us; the launch traced here: 1090 us
  waiting for transfers between devices  703 us (64%)
  matrix products  119 us (11%)
  local copies, waits for them, and re-layouts  104 us (9%)
  other arithmetic  84.3 us (8%)
  blocking collectives  58.4 us (5%)
  between operations  16.3 us (1%)
    psum x1, waiting for transfers between devices, shards(): lax.psum(ffn_part.astype(jnp.bfloat16), 'tp').astype(jnp.float32)  234 us
    psum x1, waiting for transfers between devices, shards(): dffn_in = lax.psum(dffn_part.astype(jnp.bfloat16), 'tp').astype(jnp.float32)  151 us
    psum x1, waiting for transfers between devices, shards(): lax.psum(attn_part.astype(jnp.bfloat16), 'tp').astype(jnp.float32)  148 us
    unnamed x12, waiting for transfers between devices  100 us
    unnamed x152, local copies, waits for them, and re-layouts  57.9 us
    all_gather x1, waiting for transfers between devices, shards(): lax.all_gather(reduced.astype(jnp.bfloat16), 'ctx', axis=0, tiled=True)  27.2 us
    dot_general x7, matrix products, outer_sum(): lax.dot_general(left, right, (((0,), (0,)), ((), ())), preferred_element_...  26.6 us
  transfers between devices with their start and end apart: 11, of which 9 were waited for; matrix products, arithmetic and copies ran while one was open for 13% of the time, Pallas kernels for 0%

commit v1 on v0

v1 whole, which is shorter than its diff:
```python
import functools

import jax
import jax.numpy as jnp
from jax import lax
from jax.experimental import pallas as pl
from jax.experimental.pallas import tpu as pltpu
from jax.sharding import PartitionSpec as P

EPSILON = 1e-06
NEGATIVE = -1e30
ROPE_BASE = 10000.0
F32 = jnp.float32
BF16 = jnp.bfloat16
VMEM_LIMIT = 60 * 1024 * 1024


def rms_norm(values, gain):
    return values * lax.rsqrt(jnp.mean(values * values, axis=-1, keepdims=True) + EPSILON) * gain


def rotate(values, cos_table, sin_table):
    half_dim = values.shape[-1] // 2
    turned = jnp.concatenate([-values[..., half_dim:], values[..., :half_dim]], axis=-1)
    return values * cos_table + turned * sin_table


def rotary_tables(positions, head_dim):
    inverse_freq = ROPE_BASE ** (-jnp.arange(0, head_dim, 2).astype(F32) / head_dim)
    angles = positions.astype(F32)[:, None] * inverse_freq[None, :]
    cos_half = jnp.cos(angles)
    sin_half = jnp.sin(angles)
    return (jnp.concatenate([cos_half, cos_half], -1), jnp.concatenate([sin_half, sin_half], -1))


def head_post(raw, gain, cos_table, sin_table):
    return rotate(rms_norm(raw, gain), cos_table[None, :, None, :], sin_table[None, :, None, :])


def dot(left, right, dims):
    return lax.dot_general(left, right, (dims, ((), ())), preferred_element_type=F32)


def mm(left, right):
    return dot(left, right, ((1,), (0,)))


def mm_t(left, right):
    return dot(left, right, ((1,), (1,)))


def outer_sum(left, right):
    return dot(left, right, ((0,), (0,)))


def swap_over(axis, bit):
    size = lax.axis_size(axis)
    pairs = [(i, i ^ bit) for i in range(size)]
    return lambda value: lax.ppermute(value, axis, pairs)


def bits_of(size):
    return [1 << b for b in range(size.bit_length() - 1)]


def ring_gather(value, axis, dim):
    size = lax.axis_size(axis)
    me = lax.axis_index(axis)
    pairs = [(i, (i + 1) % size) for i in range(size)]
    width = value.shape[dim]
    shape = list(value.shape)
    shape[dim] = width * size
    whole = jnp.zeros(shape, value.dtype)
    piece = value
    for step in range(size):
        if step:
            piece = lax.ppermute(piece, axis, pairs)
        whole = lax.dynamic_update_slice_in_dim(whole, piece, ((me - step) % size) * width, dim)
    return whole


def cube_gather(value, axis, dim):
    size = lax.axis_size(axis)
    me = lax.axis_index(axis)
    pieces = [(0, value)]
    for bit in reversed(bits_of(size)):
        swap = swap_over(axis, bit)
        pieces = pieces + [(mask ^ bit, swap(piece)) for mask, piece in pieces]
    width = value.shape[dim]
    shape = list(value.shape)
    shape[dim] = width * size
    whole = jnp.zeros(shape, value.dtype)
    for mask, piece in pieces:
        whole = lax.dynamic_update_slice_in_dim(whole, piece, (me ^ mask) * width, dim)
    return whole


def cube_scatter_sum(value, axis):
    size = lax.axis_size(axis)
    me = lax.axis_index(axis)
    bits = bits_of(size)
    current = value.reshape((2,) * len(bits) + value.shape[1:])
    for bit in bits:
        place = current.ndim - (value.ndim - 1) - 1
        mine = jnp.where(me & bit, 1, 0)
        keep = lax.dynamic_index_in_dim(current, mine, place, keepdims=False)
        give = lax.dynamic_index_in_dim(current, 1 - mine, place, keepdims=False)
        got = swap_over(axis, bit)(give.astype(BF16))
        current = keep + got.astype(F32)
    return current


def cube_sum(value, axis):
    for bit in bits_of(lax.axis_size(axis)):
        low = value.astype(BF16)
        value = low.astype(F32) + swap_over(axis, bit)(low).astype(F32)
    return value


def allowed_t(key_count, query_count, query_start, prefix):
    key_pos = lax.broadcasted_iota(jnp.int32, (key_count, query_count), 0)
    query_pos = query_start + lax.broadcasted_iota(jnp.int32, (key_count, query_count), 1)
    return (key_pos <= query_pos) | (key_pos < prefix)


def attend_kernel(info, prefix, q_ref, k_ref, v_ref, out_ref, lse_ref, *, heads, head_dim, tile, scale):
    seq = pl.program_id(0)
    part = pl.program_id(1)
    keys = k_ref[0]
    values = v_ref[0]
    allowed = allowed_t(keys.shape[0], tile, info[0] + part * tile, prefix[seq])
    for head in range(heads):
        lanes = slice(head * head_dim, (head + 1) * head_dim)
        query = q_ref[0, :, lanes]
        scores = mm_t(keys, query) * scale
        scores = jnp.where(allowed, scores, NEGATIVE)
        top = jnp.max(scores, axis=0, keepdims=True)
        weight = jnp.exp(scores - top)
        total = jnp.sum(weight, axis=0, keepdims=True)
        probs = weight * (1.0 / total)
        out_ref[0, :, lanes] = outer_sum(probs.astype(BF16), values)
        lse_ref[0, head : head + 1, :] = top + jnp.log(total)


def attend(info, prefix, query, keys, values, heads, head_dim):
    seqs, rows, _ = query.shape
    length = keys.shape[1]
    tile = min(256, rows)
    scale = head_dim ** (-0.5)
    return pl.pallas_call(
        functools.partial(attend_kernel, heads=heads, head_dim=head_dim, tile=tile, scale=scale),
        grid_spec=pltpu.PrefetchScalarGridSpec(
            num_scalar_prefetch=2,
            grid=(seqs, rows // tile),
            in_specs=[
                pl.BlockSpec((1, tile, heads * head_dim), lambda s, i, *_: (s, i, 0)),
                pl.BlockSpec((1, length, head_dim), lambda s, i, *_: (s, 0, 0)),
                pl.BlockSpec((1, length, head_dim), lambda s, i, *_: (s, 0, 0)),
            ],
            out_specs=[
                pl.BlockSpec((1, tile, heads * head_dim), lambda s, i, *_: (s, i, 0)),
                pl.BlockSpec((1, heads, tile), lambda s, i, *_: (s, 0, i)),
            ],
        ),
        out_shape=[
            jax.ShapeDtypeStruct((seqs, rows, heads * head_dim), F32),
            jax.ShapeDtypeStruct((seqs, heads, rows), F32),
        ],
        compiler_params=pltpu.CompilerParams(vmem_limit_bytes=VMEM_LIMIT),
        cost_estimate=pl.CostEstimate(
            flops=4 * seqs * rows * length * heads * 256,
            bytes_accessed=seqs * rows * heads * head_dim * 8,
            transcendentals=seqs * rows * length * heads,
        ),
        name="attend",
    )(info, prefix, query, keys, values)


def attend_back_kernel(
    info, prefix, q_ref, k_ref, v_ref, d_ref, lse_ref, delta_ref, dq_ref, dk_ref, dv_ref,
    *, heads, head_dim, tile, scale
):
    seq = pl.program_id(0)
    part = pl.program_id(1)

    @pl.when(part == 0)
    def _():
        dk_ref[...] = jnp.zeros_like(dk_ref)
        dv_ref[...] = jnp.zeros_like(dv_ref)

    keys = k_ref[0]
    values = v_ref[0]
    allowed = allowed_t(keys.shape[0], tile, info[0] + part * tile, prefix[seq])
    for head in range(heads):
        lanes = slice(head * head_dim, (head + 1) * head_dim)
        query = q_ref[0, :, lanes]
        dout = d_ref[0, :, lanes]
        scores = mm_t(keys, query) * scale
        probs = jnp.where(allowed, jnp.exp(scores - lse_ref[0, head : head + 1, :]), 0.0)
        dprob = mm_t(values, dout)
        dscore = (probs * (dprob - delta_ref[0, head : head + 1, :])).astype(BF16)
        dv_ref[0] += mm(probs.astype(BF16), dout)
        dk_ref[0] += mm(dscore, query) * scale
        dq_ref[0, :, lanes] = outer_sum(dscore, keys) * scale


def attend_back(info, prefix, query, keys, values, dout, lse, delta, heads, head_dim):
    seqs, rows, _ = query.shape
    length = keys.shape[1]
    tile = min(256, rows)
    scale = head_dim ** (-0.5)
    row_block = pl.BlockSpec((1, tile, heads * head_dim), lambda s, i, *_: (s, i, 0))
    key_block = pl.BlockSpec((1, length, head_dim), lambda s, i, *_: (s, 0, 0))
    stat_block = pl.BlockSpec((1, heads, tile), lambda s, i, *_: (s, 0, i))
    return pl.pallas_call(
        functools.partial(attend_back_kernel, heads=heads, head_dim=head_dim, tile=tile, scale=scale),
        grid_spec=pltpu.PrefetchScalarGridSpec(
            num_scalar_prefetch=2,
            grid=(seqs, rows // tile),
            in_specs=[row_block, key_block, key_block, row_block, stat_block, stat_block],
            out_specs=[row_block, key_block, key_block],
        ),
        out_shape=[
            jax.ShapeDtypeStruct((seqs, rows, heads * head_dim), F32),
            jax.ShapeDtypeStruct((seqs, length, head_dim), F32),
            jax.ShapeDtypeStruct((seqs, length, head_dim), F32),
        ],
        compiler_params=pltpu.CompilerParams(vmem_limit_bytes=VMEM_LIMIT),
        cost_estimate=pl.CostEstimate(
            flops=10 * seqs * rows * length * heads * 256,
            bytes_accessed=seqs * rows * heads * head_dim * 12,
            transcendentals=seqs * rows * length * heads,
        ),
        name="attend_back",
    )(info, prefix, query, keys, values, dout, lse, delta)


def shards(
    tokens, attn_gain, w_query, key_matrix, value_matrix, query_gain, key_gain, w_out, ffn_gain,
    w_gate, w_up, w_down, prefix_len, out_grad,
):
    seqs, block_len, width = tokens.shape
    rows = seqs * block_len
    tp_index = lax.axis_index("tp")
    ctx_count = lax.axis_size("ctx")
    ctx_index = lax.axis_index("ctx")
    fsdp_count = lax.axis_size("fsdp")
    head_dim = query_gain.shape[0] * fsdp_count
    q_cols = w_query.shape[1]
    kv_cols = key_matrix.shape[1]
    heads = q_cols // head_dim
    ff_cols = w_gate.shape[1]

    gains = cube_gather(
        jnp.concatenate([attn_gain, ffn_gain, query_gain, key_gain])[None], "fsdp", 0
    ).astype(F32)
    cuts = [0, attn_gain.size, 2 * attn_gain.size, 2 * attn_gain.size + query_gain.size, gains.shape[1]]
    attn_gain32, ffn_gain32, query_gain32, key_gain32 = (
        gains[:, low:high].reshape(-1) for low, high in zip(cuts, cuts[1:])
    )
    w_qkv = jnp.concatenate([w_query, key_matrix, value_matrix], axis=1)
    own_qkv = cube_gather(w_qkv, "fsdp", 0)

    full_out = cube_gather(ring_gather(w_out, "tp", 0), "fsdp", 1)
    full_gate = cube_gather(ring_gather(w_gate, "tp", 1), "fsdp", 0)
    full_up = cube_gather(ring_gather(w_up, "tp", 1), "fsdp", 0)
    full_down = cube_gather(ring_gather(w_down, "tp", 0), "fsdp", 1)
    full_qkv = cube_gather(ring_gather(w_qkv, "tp", 1), "fsdp", 0)

    query_pos = ctx_index * block_len + jnp.arange(block_len, dtype=jnp.int32)
    cos_table, sin_table = rotary_tables(query_pos, head_dim)
    inputs = tokens.astype(F32).reshape(rows, width)
    normed = rms_norm(inputs, attn_gain32).astype(BF16)
    raw = mm(normed, own_qkv)
    query_raw = raw[:, :q_cols].reshape(seqs, block_len, heads, head_dim)
    key_raw = raw[:, q_cols : q_cols + kv_cols].reshape(seqs, block_len, kv_cols // head_dim, head_dim)
    value_low = raw[:, q_cols + kv_cols :].astype(BF16).reshape(seqs, block_len, kv_cols)
    post = functools.partial(head_post, cos_table=cos_table, sin_table=sin_table)
    query_rot, query_pull = jax.vjp(post, query_raw, query_gain32)
    key_rot, key_pull = jax.vjp(post, key_raw, key_gain32)
    query_low = query_rot.astype(BF16).reshape(seqs, block_len, q_cols)
    key_low = key_rot.astype(BF16).reshape(seqs, block_len, kv_cols)
    key_value = cube_gather(jnp.concatenate([key_low, value_low], axis=2), "ctx", 1)
    keys_all = key_value[:, :, :kv_cols]
    values_all = key_value[:, :, kv_cols:]
    info = (ctx_index * block_len).astype(jnp.int32).reshape(1)
    attended, lse = attend(info, prefix_len, query_low, keys_all, values_all, heads, head_dim)
    attended_own = attended.astype(BF16).reshape(rows, q_cols)
    attended_low = ring_gather(attended_own, "tp", 1)

    residual = inputs + mm(attended_low, full_out)
    ffn_in = rms_norm(residual, ffn_gain32).astype(BF16)
    gate_proj = mm(ffn_in, full_gate)
    up_proj = mm(ffn_in, full_up)
    sig = jax.nn.sigmoid(gate_proj)
    hidden = (gate_proj * sig * up_proj).astype(BF16)
    layer_low = (residual + mm(hidden, full_down)).astype(BF16)
    grad_low = out_grad.reshape(rows, width)
    dhidden = mm_t(grad_low, full_down)
    dgate = (dhidden * up_proj * sig * (1.0 + gate_proj * (1.0 - sig))).astype(BF16)
    dup = (dhidden * gate_proj * sig).astype(BF16)

    def own_cols(values, cols):
        return lax.dynamic_slice_in_dim(values, tp_index * cols, cols, 1)

    grad_down = outer_sum(own_cols(hidden, ff_cols), grad_low)
    grad_gate = outer_sum(ffn_in, own_cols(dgate, ff_cols))
    grad_up = outer_sum(ffn_in, own_cols(dup, ff_cols))
    dffn_in = mm_t(dgate, full_gate) + mm_t(dup, full_up)
    _, ffn_pull = jax.vjp(rms_norm, residual, ffn_gain32)
    dres_norm, grad_ffn_gain = ffn_pull(dffn_in)
    dresidual = grad_low.astype(F32) + dres_norm
    dres_low = dresidual.astype(BF16)
    grad_out = outer_sum(attended_own, dres_low)
    own_out = lax.dynamic_slice_in_dim(full_out, tp_index * q_cols, q_cols, 0)
    dattended = mm_t(dres_low, own_out).astype(BF16)
    delta = jnp.sum(
        (dattended.astype(F32) * attended.reshape(rows, q_cols)).reshape(seqs, block_len, heads, head_dim),
        axis=-1,
    )
    dquery_rot, dkeys, dvalues = attend_back(
        info, prefix_len, query_low, keys_all, values_all,
        dattended.reshape(seqs, block_len, q_cols), lse, jnp.moveaxis(delta, 1, 2), heads, head_dim,
    )
    parts = jnp.concatenate([dkeys, dvalues], axis=2).reshape(seqs, ctx_count, block_len, 2 * kv_cols)
    owned = cube_scatter_sum(jnp.moveaxis(parts, 1, 0), "ctx")
    dquery_raw, grad_query_gain = query_pull(dquery_rot.reshape(query_raw.shape))
    dkey_raw, grad_key_gain = key_pull(owned[:, :, :kv_cols].reshape(key_raw.shape))
    dqkv_own = jnp.concatenate(
        [
            dquery_raw.reshape(rows, q_cols).astype(BF16),
            dkey_raw.reshape(rows, kv_cols).astype(BF16),
            owned[:, :, kv_cols:].reshape(rows, kv_cols).astype(BF16),
        ],
        axis=1,
    )
    dqkv = ring_gather(dqkv_own, "tp", 1)
    grad_qkv = outer_sum(normed, dqkv_own)
    dnormed = mm_t(dqkv, full_qkv)
    _, attn_pull = jax.vjp(rms_norm, inputs, attn_gain32)
    dinput, grad_attn_gain = attn_pull(dnormed)
    input_grad = (dresidual + dinput).astype(BF16)

    def by_rows(gradient):
        return gradient.reshape((fsdp_count, -1) + gradient.shape[1:])

    def by_cols(gradient):
        return jnp.moveaxis(gradient.reshape(gradient.shape[0], fsdp_count, -1), 1, 0)

    def settle(parts):
        return cube_sum(cube_scatter_sum(parts, "fsdp"), "ctx")

    grad_down = settle(by_cols(grad_down))
    grad_gate = settle(by_rows(grad_gate))
    grad_up = settle(by_rows(grad_up))
    grad_out = settle(by_cols(grad_out))
    grad_qkv = settle(by_rows(grad_qkv))
    head_gains = jnp.concatenate([grad_query_gain, grad_key_gain])
    head_gains = lax.psum(head_gains, "tp")
    split = query_gain.size
    gain_parts = jnp.concatenate(
        [
            grad_attn_gain.reshape(fsdp_count, -1),
            grad_ffn_gain.reshape(fsdp_count, -1),
            head_gains[:head_dim].reshape(fsdp_count, -1),
            head_gains[head_dim:].reshape(fsdp_count, -1),
        ],
        axis=1,
    )
    gain_grads = lax.psum(gain_parts, ("fsdp", "ctx"))
    gain_grads = lax.dynamic_index_in_dim(gain_grads, lax.axis_index("fsdp"), 0, keepdims=False)
    return (
        layer_low.reshape(seqs, block_len, width),
        input_grad.reshape(seqs, block_len, width),
        gain_grads[cuts[0] : cuts[1]],
        grad_qkv[:, :q_cols],
        grad_qkv[:, q_cols : q_cols + kv_cols],
        grad_qkv[:, q_cols + kv_cols :],
        gain_grads[cuts[2] : cuts[3]],
        gain_grads[cuts[3] : cuts[4]],
        grad_out,
        gain_grads[cuts[1] : cuts[2]],
        grad_gate,
        grad_up,
        grad_down,
    )


def solution(mesh):
    columns = P("fsdp", "tp")
    across = P("tp", "fsdp")
    vector = P("fsdp")
    data = P("fsdp", "ctx", None)
    return jax.shard_map(
        shards,
        mesh=mesh,
        in_specs=(
            data, vector, columns, columns, columns, vector, vector, across, vector,
            columns, columns, across, vector, data,
        ),
        out_specs=(
            data, data, vector, columns, columns, columns, vector, vector, across, vector,
            columns, columns, across,
        ),
        check_vma=False,
    )
```

time: 1100 us -> 547 us (0.50)
  waiting for transfers between devices: 703 us -> 162 us
  starting transfers between devices: 0.44 us -> 37.2 us
  Pallas kernels: 0 us -> 31.1 us
  other arithmetic: 84.3 us -> 55.3 us
  matrix products: 119 us -> 93 us
  blocking collectives: 58.4 us -> 34.8 us
  local copies, waits for them, and re-layouts: 104 us -> 122 us
  between operations: 16.3 us -> 2.82 us
    psum x3 -> x0, waiting for transfers between devices: 533 us -> none  [the longest x1 234 us: shards(): lax.psum(ffn_part.astype(jnp.bfloat16), 'tp').astype(jnp.float32)]
    ppermute x0 -> x59, waiting for transfers between devices: none -> 162 us  [the longest x38 88.8 us: swap_over(): return lambda value: lax.ppermute(value, axis, pairs)]
    unnamed x12 -> x0, waiting for transfers between devices: 100 us -> none
    all_gather x6 -> x0, waiting for transfers between devices: 59.2 us -> none  [the longest x1 27.2 us: shards(): lax.all_gather(reduced.astype(jnp.bfloat16), 'ctx', axis=0, tiled=True)]
    unnamed x152 -> x138, local copies, waits for them, and re-layouts: 57.9 us -> 6.68 us
    dynamic_update_slice x0 -> x55, local copies, waits for them, and re-layouts: none -> 51.1 us  [the longest x29 28.1 us: cube_gather(): lax.dynamic_update_slice_in_dim(whole, piece, (me ^ mask) * width, dim)]
    all_gather x6 -> x0, blocking collectives: 37.7 us -> none  [the longest x1 8.19 us: shards(): lax.all_gather(key_matrix, 'fsdp', axis=0, tiled=True)]
    ppermute x0 -> x59, starting transfers between devices: none -> 37.2 us  [the longest x38 20 us: swap_over(): return lambda value: lax.ppermute(value, axis, pairs)]
  transfers between devices with their start and end apart: 11 -> 59, of which waited for: 9 -> 24; matrix products, arithmetic and copies ran while one was open for 13% -> 44% of each run, Pallas kernels for 0% -> 6%
where the time goes in v1:
time: 547 us; the launch traced here: 539 us
  waiting for transfers between devices  162 us (30%)
  local copies, waits for them, and re-layouts  122 us (22%)
  matrix products  93 us (17%)
  other arithmetic  55.3 us (10%)
  starting transfers between devices  37.2 us (7%)
  blocking collectives  34.8 us (6%)
  Pallas kernels  31.1 us (6%)
    dot_general x15, matrix products, dot(): lax.dot_general(left, right, (dims, ((), ())), preferred_element_type=F32)  93 us
    ppermute x38, waiting for transfers between devices, swap_over(): return lambda value: lax.ppermute(value, axis, pairs)  88.8 us
    ppermute x21, waiting for transfers between devices, ring_gather(): piece = lax.ppermute(piece, axis, pairs)  73.7 us
    dynamic_update_slice x29, local copies, waits for them, and re-layouts, cube_gather(): lax.dynamic_update_slice_in_dim(whole, piece, (me ^ mask) * width, dim)  28.1 us
    dynamic_update_slice x26, local copies, waits for them, and re-layouts, ring_gather(): lax.dynamic_update_slice_in_dim(whole, piece, (me - step) % size * width,...  23 us
    psum x1, blocking collectives, shards(): gain_grads = lax.psum(gain_parts, ('fsdp', 'ctx'))  22.9 us
    ppermute x38, starting transfers between devices, swap_over(): return lambda value: lax.ppermute(value, axis, pairs)  20 us
    dot_general x3, local copies, waits for them, and re-layouts, dot(): lax.dot_general(left, right, (dims, ((), ())), preferred_element_type=F32)  19.3 us
  transfers between devices with their start and end apart: 59, of which 24 were waited for; matrix products, arithmetic and copies ran while one was open for 44% of the time, Pallas kernels for 6%

profile of v1, /device:TPU:0, one launch (start us, length us, event | category | flops | bytes accessed | tf_op | source)
XLA Modules:
  0.0 538.5 jit_solution(8403169786433480814)
XLA Ops:
  32.4 6.5 %copy.203 = bf16[2048,1024]{1,0:T(8,128)(2,1)} copy(bf16[2048,1024]{0,1:T(8,128)(2,1)} %bitcast.221) | data formatting | bytes 8388608 | tf_op jit(solution)/shard_map/dot_general | solution.py:41
  48.7 6.3 %copy.199 = bf16[2048,1024]{1,0:T(8,128)(2,1)} copy(bf16[2048,1024]{0,1:T(8,128)(2,1)} %bitcast.220) | data formatting | bytes 8388608 | tf_op jit(solution)/shard_map/dot_general | solution.py:41
  98.8 12.2 %collective-permute-done.12 = bf16[256,512]{1,0:T(8,128)(2,1)S(1)} collective-permute-done((bf16[256,512]{1,0:T(8,128)(2,1)S(1)}, bf16[256,512]{1,0:T(8,128)(2,1)S(1)}, u32[]{:S(2)}, u32[]{:S(2)}) %collective-permute-start.12) | collective-permute-done | bytes 262176 | tf_op jit(solution)/shard_map/ppermute | solution.py:77
  140.5 14.4 %attend.1 = (f32[2,512,256]{2,1,0:T(8,128)}, f32[2,4,512]{2,1,0:T(4,128)}) custom-call(s32[1]{0:T(128)} %bitcast.1.info, s32[2]{0:T(128)} %prefix.3, bf16[2,512,256]{2,1,0:T(8,128)(2,1)} %add_convert_fusion.1.q_ref, bf16[2,1024,64]{2,1,0:T(8,128)(2,1)} %get-tuple-element.120.k_ref, bf16[2,1024,64]{2,1,0:T(8,128)(2,1)} %get-tuple-element.119.v_ref), custom_call_target="tpu_custom_call" | custom-call | flops 4294967296 | bytes 2097152 | tf_op jit(solution)/shard_map/attend/pallas_call | solution.py:150
  177.2 8.1 %collective-permute-done.19 = bf16[512,1024]{1,0:T(8,128)(2,1)} collective-permute-done((bf16[512,1024]{1,0:T(8,128)(2,1)S(1)}, bf16[512,1024]{1,0:T(8,128)(2,1)}, u32[]{:S(2)}, u32[]{:S(2)}) %collective-permute-start.19) | collective-permute-done | bytes 1048608 | tf_op jit(solution)/shard_map/ppermute | solution.py:59
  190.1 17.6 %collective-permute-done.31 = bf16[1024,512]{1,0:T(8,128)(2,1)} collective-permute-done((bf16[1024,512]{1,0:T(8,128)(2,1)}, bf16[1024,512]{1,0:T(8,128)(2,1)}, u32[]{:S(2)}, u32[]{:S(2)}) %collective-permute-start.31) | collective-permute-done | bytes 1048608 | tf_op jit(solution)/shard_map/ppermute | solution.py:59
  215.2 8.9 %collective-permute-done.8 = bf16[1024,256]{1,0:T(8,128)(2,1)S(1)} collective-permute-done((bf16[1024,256]{1,0:T(8,128)(2,1)S(1)}, bf16[1024,256]{1,0:T(8,128)(2,1)S(1)}, u32[]{:S(2)}, u32[]{:S(2)}) %collective-permute-start.8) | collective-permute-done | bytes 524320 | tf_op jit(solution)/shard_map/ppermute | solution.py:77
  232.3 7.0 %collective-permute-done.9 = bf16[1024,256]{1,0:T(8,128)(2,1)S(1)} collective-permute-done((bf16[1024,256]{1,0:T(8,128)(2,1)S(1)}, bf16[1024,256]{1,0:T(8,128)(2,1)S(1)}, u32[]{:S(2)}, u32[]{:S(2)}) %collective-permute-start.9) | collective-permute-done | bytes 524320 | tf_op jit(solution)/shard_map/ppermute | solution.py:77
  239.4 23.9 %collective-permute-done.41 = bf16[512,1536]{1,0:T(8,128)(2,1)} collective-permute-done((bf16[512,1536]{1,0:T(8,128)(2,1)S(1)}, bf16[512,1536]{1,0:T(8,128)(2,1)}, u32[]{:S(2)}, u32[]{:S(2)}) %collective-permute-start.41) | collective-permute-done | bytes 1572896 | tf_op jit(solution)/shard_map/ppermute | solution.py:59
  274.7 8.9 %fusion.69 = f32[1024,1024]{1,0:T(8,128)} fusion(bf16[1024,2048]{1,0:T(8,128)(2,1)S(1)} %multiply_convert_fusion, bf16[2048,1024]{1,0:T(8,128)(2,1)} %constant_dynamic-update-slice_fusion.28), kind=kOutput, calls=%fused_computation.214 | convolution fusion | flops 4294967296 | bytes 12582912 | tf_op jit(solution)/shard_map/dot_general | solution.py:41
  285.0 6.1 %fusion.70 = f32[1024,1024]{0,1:T(8,128)} fusion(bf16[1024,2048]{1,0:T(8,128)(2,1)S(1)} %constant_dynamic-update-slice_fusion.12, bf16[1024,2048]{1,0:T(8,128)(2,1)S(1)} %bitcast.222), kind=kOutput, calls=%fused_computation.215 | convolution fusion | flops 4294967296 | bytes 12582912 | tf_op jit(solution)/shard_map/dot_general | solution.py:41
  292.4 9.6 %fusion.11 = (bf16[1024,1024]{1,0:T(8,128)(2,1)}, bf16[1024,1024]{1,0:T(8,128)(2,1)S(1)}, bf16[1024,1024]{1,0:T(8,128)(2,1)S(1)}) fusion(f32[1024,1024]{0,1:T(8,128)} %fusion.70, f32[1024,1024]{1,0:T(8,128)} %fusion.69, bf16[1024,2048]{1,0:T(8,128)(2,1)S(1)} %multiply_convert_fusion, bf16[2048,1024]{1,0:T(8,128)(2,1)S(1)} %constant_dynamic-update-slice_fusion.20), kind=kOutput, calls=%fused_computation.25 | convolution fusion | flops 4311744512 | bytes 23068672 | tf_op jit(solution)/shard_map/dot_general | solution.py:41
  302.0 6.8 %fusion.71 = f32[1024,2048]{1,0:T(8,128)} fusion(bf16[1024,1024]{1,0:T(8,128)(2,1)S(1)} %get-tuple-element.105, bf16[2048,1024]{1,0:T(8,128)(2,1)S(1)} %constant_dynamic-update-slice_fusion.20), kind=kOutput, calls=%fused_computation.216 | convolution fusion | flops 4294967296 | bytes 14680064 | tf_op jit(solution)/shard_map/dot_general | solution.py:41
  310.3 9.1 %add_convert_fusion = bf16[1024,2048]{1,0:T(8,128)(2,1)} fusion(f32[1024,2048]{1,0:T(8,128)S(1)} %get-tuple-element.136, bf16[1024,1024]{1,0:T(8,128)(2,1)S(1)} %get-tuple-element.106, bf16[1024,2048]{1,0:T(8,128)(2,1)} %copy-done.16), kind=kOutput, calls=%fused_computation.18 | convolution fusion | flops 4299161600 | bytes 18874368 | tf_op jit(solution)/shard_map/dot_general | solution.py:41
  326.7 11.2 %multiply_reduce_fusion = (f32[2048]{0:T(1024)S(1)}, f32[1024]{0:T(1024)S(1)}, f32[1024,2048]{1,0:T(8,128)}) fusion(f32[1024,2048]{1,0:T(8,128)S(1)} %get-tuple-element.136, f32[1024]{0:T(1024)S(1)} %fusion.57, f32[2048]{0:T(1024)S(1)} %bitcast.257, f32[1024,2048]{1,0:T(8,128)} %fusion.71, bf16[1024,1024]{1,0:T(8,128)(2,1)S(1)} %copy-done.64, ...), kind=kOutput, calls=%fused_computation.16 | convolution fusion | flops 4309644288 | bytes 31481856 | tf_op jit(solution)/shard_map/dot_general | solution.py:41
  337.9 8.7 %convert_bitcast_fusion = (bf16[2048,1024]{0,1:T(8,128)(2,1)}, f32[1024,2048]{1,0:T(8,128)}) fusion(f32[1024,2048]{1,0:T(8,128)S(1)} %get-tuple-element.136, f32[1024]{0:T(1024)S(1)} %multiply_multiply_fusion.5, f32[1024]{0:T(1024)S(1)} %fusion.57, f32[1024,2048]{1,0:T(8,128)} %get-tuple-element.137, f32[2048]{0:T(1024)S(1)} %bitcast.258, ...), kind=kLoop, calls=%fused_computation.31 | loop fusion | flops 16777216 | bytes 33570816 | tf_op jit(solution)/shard_map/dot_general | solution.py:41
  346.6 6.5 %copy.201 = bf16[2048,1024]{1,0:T(8,128)(2,1)} copy(bf16[2048,1024]{0,1:T(8,128)(2,1)} %get-tuple-element.96) | data formatting | bytes 8388608 | tf_op jit(solution)/shard_map/dot_general | solution.py:41
  363.1 16.7 %attend_back.1 = (f32[2,512,256]{2,1,0:T(8,128)}, f32[2,1024,64]{2,1,0:T(8,128)}, f32[2,1024,64]{2,1,0:T(8,128)}) custom-call(s32[1]{0:T(128)} %bitcast.1.info, s32[2]{0:T(128)} %prefix.3, bf16[2,512,256]{2,1,0:T(8,128)(2,1)} %add_convert_fusion.1.q_ref, bf16[2,1024,64]{2,1,0:T(8,128)(2,1)} %get-tuple-element.120.k_ref, ...), custom_call_target="tpu_custom_call" | custom-call | flops 10737418240 | bytes 3145728 | tf_op jit(solution)/shard_map/attend_back/pallas_call | solution.py:215
  401.5 11.9 %psum.14 = f32[128]{0:T(128)S(1)} all-reduce(f32[128]{0:T(128)S(1)} %pad_maximum_fusion.7), channel_id=1, replica_groups=mesh['fsdp'=4,'ctx'=2,'tp'=4] {'tp'}, use_global_device_ids=true, to_apply=%region_13.14 | all-reduce | flops 128 | bytes 1024 | tf_op jit(solution)/shard_map/psum | solution.py:359
  464.6 7.1 %collective-permute-done.36 = bf16[1024,384]{0,1:T(8,128)(2,1)S(1)} collective-permute-done((bf16[1024,384]{0,1:T(8,128)(2,1)S(1)}, bf16[1024,384]{0,1:T(8,128)(2,1)S(1)}, u32[]{:S(2)}, u32[]{:S(2)}) %collective-permute-start.36) | collective-permute-done | bytes 786464 | tf_op jit(solution)/shard_map/ppermute | solution.py:77
  478.0 10.6 %collective-permute-done.37 = bf16[1024,384]{0,1:T(8,128)(2,1)S(1)} collective-permute-done((bf16[1024,384]{0,1:T(8,128)(2,1)S(1)}, bf16[1024,384]{0,1:T(8,128)(2,1)S(1)}, u32[]{:S(2)}, u32[]{:S(2)}) %collective-permute-start.37) | collective-permute-done | bytes 786464 | tf_op jit(solution)/shard_map/ppermute | solution.py:77
  489.6 13.9 %fusion.6 = (f32[2048]{0:T(1024)S(1)}, f32[1024]{0:T(1024)S(1)}, f32[1024,2048]{1,0:T(8,128)}) fusion(bf16[2,512,2048]{2,1,0:T(8,128)(2,1)} %param.14, f32[1024]{0:T(1024)S(1)} %copy-done.59, f32[2048]{0:T(1024)S(1)} %bitcast.254, bf16[1024,1536]{0,1:T(8,128)(2,1)} %constant_dynamic-update-slice_fusion.8, ...), kind=kOutput, calls=%fused_computation.13 | convolution fusion | flops 6457127936 | bytes 22044672 | tf_op jit(solution)/shard_map/dot_general | solution.py:41
  503.6 22.9 %psum.15 = f32[4,1056]{1,0:T(4,128)S(1)} all-reduce(f32[4,1056]{1,0:T(4,128)S(1)} %concatenate.55), channel_id=1, replica_groups=mesh['fsdp'=4,'ctx'=2,'tp'=4] {'fsdp','ctx'}, use_global_device_ids=true, to_apply=%region_14.15 | all-reduce | flops 4224 | bytes 33792 | tf_op jit(solution)/shard_map/psum | solution.py:370
  527.8 10.3 %fusion.2 = bf16[1024,2048]{1,0:T(8,128)(2,1)} fusion(f32[1024,2048]{1,0:T(8,128)} %get-tuple-element.97, bf16[2,512,2048]{2,1,0:T(8,128)(2,1)} %param.14, f32[1024,2048]{1,0:T(8,128)} %get-tuple-element.140, f32[1024]{0:T(1024)S(1)} %multiply_multiply_fusion.3, f32[2048]{0:T(1024)S(1)} %bitcast.255, f32[1024]{0:T(1024)S(1)} %copy-done.59), kind=kLoop, calls=%fused_computation.4 | loop fusion | flops 16777216 | bytes 25182208 | tf_op jit(solution)/shard_map/convert_element_type | solution.py:342
  (437 shorter events, 270.4 us)
Async XLA Ops:
  4.6 62.2 %collective-permute-start.3 = (bf16[512,384]{1,0:T(8,128)(2,1)}, bf16[512,384]{1,0:T(8,128)(2,1)}, u32[]{:S(2)}, u32[]{:S(2)}) collective-permute-start(bf16[512,384]{1,0:T(8,128)(2,1)} %get-tuple-element.99), channel_id=1, source_target_pairs={{0,16},{8,24},{16,0},{24,8},{1,17},{9,25},{17,1},{25,9},{2,18},{10... | collective-permute-start | bytes 1179656 | tf_op jit(solution)/shard_map/ppermute | solution.py:59
  7.5 61.0 %collective-permute-start.4 = (bf16[512,384]{1,0:T(8,128)(2,1)}, bf16[512,384]{1,0:T(8,128)(2,1)}, u32[]{:S(2)}, u32[]{:S(2)}) collective-permute-start(bf16[512,384]{1,0:T(8,128)(2,1)} %get-tuple-element.99), channel_id=1, source_target_pairs={{0,8},{8,0},{16,24},{24,16},{1,9},{9,1},{17,25},{25,17},{2,10},{10... | collective-permute-start | bytes 1179656 | tf_op jit(solution)/shard_map/ppermute | solution.py:59
  11.0 44.1 %collective-permute-start.10 = (bf16[256,512]{1,0:T(8,128)(2,1)}, bf16[256,512]{1,0:T(8,128)(2,1)}, u32[]{:S(2)}, u32[]{:S(2)}) collective-permute-start(bf16[256,512]{1,0:T(8,128)(2,1)} %param.21), channel_id=1, source_target_pairs={{0,1},{1,2},{2,3},{3,0},{4,5},{5,6},{6,7},{7,4},{8,9},{9,10},{10,1... | collective-permute-start | bytes 786440 | tf_op jit(solution)/shard_map/ppermute | solution.py:77
  74.6 37.3 %collective-permute-start.5 = (bf16[512,384]{1,0:T(8,128)(2,1)}, bf16[512,384]{1,0:T(8,128)(2,1)S(1)}, u32[]{:S(2)}, u32[]{:S(2)}) collective-permute-start(bf16[512,384]{1,0:T(8,128)(2,1)} %collective-permute-done.3), channel_id=1, source_target_pairs={{0,8},{8,0},{16,24},{24,16},{1,9},{9,1},{17,25},{25,17},{2,10},{10... | collective-permute-start | bytes 1179656 | tf_op jit(solution)/shard_map/ppermute | solution.py:59
  80.1 56.7 %collective-permute-start.39 = (bf16[512,384]{1,0:T(8,128)(2,1)}, bf16[512,384]{1,0:T(8,128)(2,1)}, u32[]{:S(2)}, u32[]{:S(2)}) collective-permute-start(bf16[512,384]{1,0:T(8,128)(2,1)} %collective-permute-done.38), channel_id=1, source_target_pairs={{0,1},{1,2},{2,3},{3,0},{4,5},{5,6},{6,7},{7,4},{8,9},{9,10},{10,1... | collective-permute-start | bytes 1179656 | tf_op jit(solution)/shard_map/ppermute | solution.py:77
  91.4 64.8 %collective-permute-start.18 = (bf16[512,256]{1,0:T(8,128)(2,1)}, bf16[512,256]{1,0:T(8,128)(2,1)}, u32[]{:S(2)}, u32[]{:S(2)}) collective-permute-start(bf16[512,256]{1,0:T(8,128)(2,1)} %collective-permute-done.17), channel_id=1, source_target_pairs={{0,1},{1,2},{2,3},{3,0},{4,5},{5,6},{6,7},{7,4},{8,9},{9,10},{10,1... | collective-permute-start | bytes 786440 | tf_op jit(solution)/shard_map/ppermute | solution.py:77
  97.1 61.9 %collective-permute-start.30 = (bf16[256,512]{1,0:T(8,128)(2,1)}, bf16[256,512]{1,0:T(8,128)(2,1)}, u32[]{:S(2)}, u32[]{:S(2)}) collective-permute-start(bf16[256,512]{1,0:T(8,128)(2,1)} %collective-permute-done.29), channel_id=1, source_target_pairs={{0,1},{1,2},{2,3},{3,0},{4,5},{5,6},{6,7},{7,4},{8,9},{9,10},{10,1... | collective-permute-start | bytes 786440 | tf_op jit(solution)/shard_map/ppermute | solution.py:77
  111.0 48.1 %collective-permute-start.24 = (bf16[512,256]{1,0:T(8,128)(2,1)}, bf16[512,256]{1,0:T(8,128)(2,1)}, u32[]{:S(2)}, u32[]{:S(2)}) collective-permute-start(bf16[512,256]{1,0:T(8,128)(2,1)} %collective-permute-done.23), channel_id=1, source_target_pairs={{0,1},{1,2},{2,3},{3,0},{4,5},{5,6},{6,7},{7,4},{8,9},{9,10},{10,1... | collective-permute-start | bytes 786440 | tf_op jit(solution)/shard_map/ppermute | solution.py:77
  136.8 35.3 %collective-permute-start.13 = (bf16[1024,512]{1,0:T(8,128)(2,1)}, bf16[1024,512]{1,0:T(8,128)(2,1)S(1)}, u32[]{:S(2)}, u32[]{:S(2)}) collective-permute-start(bf16[1024,512]{1,0:T(8,128)(2,1)} %constant_dynamic-update-slice_fusion.40), channel_id=1, source_target_pairs={{0,16},{8,24},{16,0},{24,8},{1,17},{9,25},{17,1},{25,9},{2,18},{10... | collective-permute-start | bytes 3145736 | tf_op jit(solution)/shard_map/ppermute | solution.py:59
  169.6 38.1 %collective-permute-start.31 = (bf16[1024,512]{1,0:T(8,128)(2,1)}, bf16[1024,512]{1,0:T(8,128)(2,1)}, u32[]{:S(2)}, u32[]{:S(2)}) collective-permute-start(bf16[1024,512]{1,0:T(8,128)(2,1)} %constant_dynamic-update-slice_fusion.16), channel_id=1, source_target_pairs={{0,16},{8,24},{16,0},{24,8},{1,17},{9,25},{17,1},{25,9},{2,18},{10... | collective-permute-start | bytes 3145736 | tf_op jit(solution)/shard_map/ppermute | solution.py:59
  172.2 35.7 %collective-permute-start.32 = (bf16[1024,512]{1,0:T(8,128)(2,1)}, bf16[1024,512]{1,0:T(8,128)(2,1)S(1)}, u32[]{:S(2)}, u32[]{:S(2)}) collective-permute-start(bf16[1024,512]{1,0:T(8,128)(2,1)} %constant_dynamic-update-slice_fusion.16), channel_id=1, source_target_pairs={{0,8},{8,0},{16,24},{24,16},{1,9},{9,1},{17,25},{25,17},{2,10},{10... | collective-permute-start | bytes 3145736 | tf_op jit(solution)/shard_map/ppermute | solution.py:59
  175.6 54.6 %collective-permute-start.25 = (bf16[512,1024]{1,0:T(8,128)(2,1)}, bf16[512,1024]{1,0:T(8,128)(2,1)}, u32[]{:S(2)}, u32[]{:S(2)}) collective-permute-start(bf16[512,1024]{1,0:T(8,128)(2,1)} %constant_dynamic-update-slice_fusion.24), channel_id=1, source_target_pairs={{0,16},{8,24},{16,0},{24,8},{1,17},{9,25},{17,1},{25,9},{2,18},{10... | collective-permute-start | bytes 3145736 | tf_op jit(solution)/shard_map/ppermute | solution.py:59
  185.3 78.1 %collective-permute-start.41 = (bf16[512,1536]{1,0:T(8,128)(2,1)S(1)}, bf16[512,1536]{1,0:T(8,128)(2,1)}, u32[]{:S(2)}, u32[]{:S(2)}) collective-permute-start(bf16[512,1536]{1,0:T(8,128)(2,1)S(1)} %constant_dynamic-update-slice_fusion.4), channel_id=1, source_target_pairs={{0,16},{8,24},{16,0},{24,8},{1,17},{9,25},{17,1},{25,9},{2,18},{10... | collective-permute-start | bytes 4718600 | tf_op jit(solution)/shard_map/ppermute | solution.py:59
  190.1 41.5 %collective-permute-start.26 = (bf16[512,1024]{1,0:T(8,128)(2,1)}, bf16[512,1024]{1,0:T(8,128)(2,1)S(1)}, u32[]{:S(2)}, u32[]{:S(2)}) collective-permute-start(bf16[512,1024]{1,0:T(8,128)(2,1)} %constant_dynamic-update-slice_fusion.24), channel_id=1, source_target_pairs={{0,8},{8,0},{16,24},{24,16},{1,9},{9,1},{17,25},{25,17},{2,10},{10... | collective-permute-start | bytes 3145736 | tf_op jit(solution)/shard_map/ppermute | solution.py:59
  207.7 58.3 %collective-permute-start.42 = (bf16[512,1536]{1,0:T(8,128)(2,1)S(1)}, bf16[512,1536]{1,0:T(8,128)(2,1)S(1)}, u32[]{:S(2)}, u32[]{:S(2)}) collective-permute-start(bf16[512,1536]{1,0:T(8,128)(2,1)S(1)} %constant_dynamic-update-slice_fusion.4), channel_id=1, source_target_pairs={{0,8},{8,0},{16,24},{24,16},{1,9},{9,1},{17,25},{25,17},{2,10},{10... | collective-permute-start | bytes 4718600 | tf_op jit(solution)/shard_map/ppermute | solution.py:59
  230.2 37.6 %collective-permute-start.15 = (bf16[1024,512]{1,0:T(8,128)(2,1)S(1)}, bf16[1024,512]{1,0:T(8,128)(2,1)S(1)}, u32[]{:S(2)}, u32[]{:S(2)}) collective-permute-start(bf16[1024,512]{1,0:T(8,128)(2,1)S(1)} %collective-permute-done.13), channel_id=1, source_target_pairs={{0,8},{8,0},{16,24},{24,16},{1,9},{9,1},{17,25},{25,17},{2,10},{10... | collective-permute-start | bytes 3145736 | tf_op jit(solution)/shard_map/ppermute | solution.py:59
  231.6 42.1 %collective-permute-start.21 = (bf16[512,1024]{1,0:T(8,128)(2,1)}, bf16[512,1024]{1,0:T(8,128)(2,1)S(1)}, u32[]{:S(2)}, u32[]{:S(2)}) collective-permute-start(bf16[512,1024]{1,0:T(8,128)(2,1)} %collective-permute-done.19), channel_id=1, source_target_pairs={{0,8},{8,0},{16,24},{24,16},{1,9},{9,1},{17,25},{25,17},{2,10},{10... | collective-permute-start | bytes 3145736 | tf_op jit(solution)/shard_map/ppermute | solution.py:59
  239.4 44.2 %collective-permute-start.33 = (bf16[1024,512]{1,0:T(8,128)(2,1)}, bf16[1024,512]{1,0:T(8,128)(2,1)}, u32[]{:S(2)}, u32[]{:S(2)}) collective-permute-start(bf16[1024,512]{1,0:T(8,128)(2,1)} %collective-permute-done.31), channel_id=1, source_target_pairs={{0,8},{8,0},{16,24},{24,16},{1,9},{9,1},{17,25},{25,17},{2,10},{10... | collective-permute-start | bytes 3145736 | tf_op jit(solution)/shard_map/ppermute | solution.py:59
  266.1 205.7 %collective-permute-start.43 = (bf16[512,1536]{1,0:T(8,128)(2,1)}, bf16[512,1536]{1,0:T(8,128)(2,1)}, u32[]{:S(2)}, u32[]{:S(2)}) collective-permute-start(bf16[512,1536]{1,0:T(8,128)(2,1)} %collective-permute-done.41), channel_id=1, source_target_pairs={{0,8},{8,0},{16,24},{24,16},{1,9},{9,1},{17,25},{25,17},{2,10},{10... | collective-permute-start | bytes 4718600 | tf_op jit(solution)/shard_map/ppermute | solution.py:59
  321.8 93.9 %collective-permute-start.56 = (bf16[2,256,512]{2,1,0:T(8,128)(2,1)}, bf16[2,256,512]{2,1,0:T(8,128)(2,1)}, u32[]{:S(2)}, u32[]{:S(2)}) collective-permute-start(bf16[2,256,512]{2,1,0:T(8,128)(2,1)} %fusion.29), channel_id=1, source_target_pairs={{0,8},{8,0},{16,24},{24,16},{1,9},{9,1},{17,25},{25,17},{2,10},{10... | collective-permute-start | bytes 1572872 | tf_op jit(solution)/shard_map/ppermute | solution.py:59
  322.6 94.7 %collective-permute-start.53 = (bf16[2,512,256]{2,1,0:T(8,128)(2,1)}, bf16[2,512,256]{2,1,0:T(8,128)(2,1)}, u32[]{:S(2)}, u32[]{:S(2)}) collective-permute-start(bf16[2,512,256]{2,1,0:T(8,128)(2,1)} %fusion.28), channel_id=1, source_target_pairs={{0,8},{8,0},{16,24},{24,16},{1,9},{9,1},{17,25},{25,17},{2,10},{10... | collective-permute-start | bytes 1572872 | tf_op jit(solution)/shard_map/ppermute | solution.py:59
  326.6 92.3 %collective-permute-start.50 = (bf16[2,512,256]{2,1,0:T(8,128)(2,1)}, bf16[2,512,256]{2,1,0:T(8,128)(2,1)}, u32[]{:S(2)}, u32[]{:S(2)}) collective-permute-start(bf16[2,512,256]{2,1,0:T(8,128)(2,1)} %fusion.27), channel_id=1, source_target_pairs={{0,8},{8,0},{16,24},{24,16},{1,9},{9,1},{17,25},{25,17},{2,10},{10... | collective-permute-start | bytes 1572872 | tf_op jit(solution)/shard_map/ppermute | solution.py:59
  415.7 29.2 %collective-permute-start.44 = (bf16[2,512,384]{1,2,0:T(8,128)(2,1)S(1)}, bf16[2,512,384]{1,2,0:T(8,128)(2,1)S(1)}, u32[]{:S(2)}, u32[]{:S(2)}) collective-permute-start(bf16[2,512,384]{1,2,0:T(8,128)(2,1)S(1)} %fusion.21), channel_id=1, source_target_pairs={{0,8},{8,0},{16,24},{24,16},{1,9},{9,1},{17,25},{25,17},{2,10},{10... | collective-permute-start | bytes 2359304 | tf_op jit(solution)/shard_map/ppermute | solution.py:59
  417.3 36.7 %collective-permute-start.35 = (bf16[1024,384]{0,1:T(8,128)(2,1)S(1)}, bf16[1024,384]{0,1:T(8,128)(2,1)S(1)}, u32[]{:S(2)}, u32[]{:S(2)}) collective-permute-start(bf16[1024,384]{0,1:T(8,128)(2,1)S(1)} %get-tuple-element.115), channel_id=1, source_target_pairs={{0,1},{1,2},{2,3},{3,0},{4,5},{5,6},{6,7},{7,4},{8,9},{9,10},{10,1... | collective-permute-start | bytes 2359304 | tf_op jit(solution)/shard_map/ppermute | solution.py:77
  (100 other events, 1556.5 us)

commit v2 on v1

v2 whole, which is shorter than its diff:
```python
import functools

import jax
import jax.numpy as jnp
from jax import lax
from jax.experimental import pallas as pl
from jax.experimental.pallas import tpu as pltpu
from jax.sharding import PartitionSpec as P

EPSILON = 1e-06
NEGATIVE = -1e30
ROPE_BASE = 10000.0
F32 = jnp.float32
BF16 = jnp.bfloat16
VMEM_LIMIT = 60 * 1024 * 1024
ANY = pl.BlockSpec(memory_space=pl.ANY)


def dot(left, right, dims, precision=None):
    return lax.dot_general(
        left, right, (dims, ((), ())), precision=precision, preferred_element_type=F32
    )


def mm(left, right):
    return dot(left, right, ((1,), (0,)))


def mm_t(left, right):
    return dot(left, right, ((1,), (1,)))


def outer_sum(left, right):
    return dot(left, right, ((0,), (0,)))


def params():
    return pltpu.CompilerParams(vmem_limit_bytes=VMEM_LIMIT)


def cost(flops, nbytes, exps=0):
    return pl.CostEstimate(flops=int(flops), bytes_accessed=int(nbytes), transcendentals=int(exps))


def rotary_tables(positions, head_dim):
    inverse_freq = ROPE_BASE ** (-jnp.arange(0, head_dim, 2).astype(F32) / head_dim)
    angles = positions.astype(F32)[:, None] * inverse_freq[None, :]
    return (jnp.cos(angles), jnp.sin(angles))


def swap(value, axis, bit):
    return lax.ppermute(value, axis, [(i, i ^ bit) for i in range(lax.axis_size(axis))])


def bits_of(size):
    return [1 << b for b in range(size.bit_length() - 1)]


def ring(value, axis):
    size = lax.axis_size(axis)
    pieces = [value]
    for _ in range(size - 1):
        pieces.append(lax.ppermute(pieces[-1], axis, [(i, (i + 1) % size) for i in range(size)]))
    return pieces


def cube(value, axis):
    stacked = value[None]
    for bit in bits_of(lax.axis_size(axis)):
        stacked = jnp.concatenate([stacked, swap(stacked, axis, bit)], axis=0)
    return stacked


def cube_sum(value, axis):
    for bit in bits_of(lax.axis_size(axis)):
        low = value.astype(BF16)
        value = low.astype(F32) + swap(low, axis, bit).astype(F32)
    return value


def cube_own(value, axis):
    for bit in reversed(bits_of(lax.axis_size(axis))):
        half = value.shape[0] // 2
        value = value[:half] + swap(value[half:].astype(BF16), axis, bit).astype(F32)
    return value[0]


def after(value, *others):
    return lax.optimization_barrier((value,) + others)[0]


def place_of():
    return jnp.stack(
        [lax.axis_index("fsdp"), lax.axis_index("ctx"), lax.axis_index("tp")]
    ).astype(jnp.int32)


class Pieces:
    def __init__(self, arrays, listing, shape, dims):
        self.arrays = arrays
        self.listing = listing
        self.shape = shape
        self.dims = dims

    def copies(self, place, refs, target, only_own=False):
        for number, index, where in self.listing:
            spot = where(place)
            if spot is None:
                continue
            row, col, own = spot
            if only_own and not own:
                continue
            rows, cols = self.shape
            if only_own:
                row = row - place[2] * self.dims
            yield (
                refs[number].at[index],
                target.at[pl.ds(pl.multiple_of(row, rows), rows), pl.ds(pl.multiple_of(col, cols), cols)],
            )


def gathered_columns(stack, lead, fsdp_count, tp_count, shape):
    rows, cols = shape
    listing = []
    for f in range(fsdp_count):
        for t in range(tp_count):
            listing.append(
                (0, (f * tp_count + t,) + lead, lambda place, f=f, t=t: (f * rows, t * cols, False))
            )
    return Pieces([stack], listing, shape, rows)


def gathered_rows(stack, lead, fsdp_count, tp_count, shape):
    rows, cols = shape
    listing = []
    for f in range(fsdp_count):
        for t in range(tp_count):
            listing.append(
                (0, (f * tp_count + t,) + lead, lambda place, f=f, t=t: (t * rows, f * cols, False))
            )
    return Pieces([stack], listing, shape, rows)


def travelled_rows(shard, tp_count):
    rows = shard.shape[0] // 2
    cols = shard.shape[1]
    half = lax.dynamic_slice_in_dim(shard, lax.axis_index("ctx") * rows, rows, 0)
    pair = jnp.stack([half, swap(half, "fsdp", 2)])
    mine = jnp.stack(ring(pair, "tp"))
    other = swap(mine, "ctx", 1)
    arrays = [mine, other, swap(mine, "fsdp", 1), swap(other, "fsdp", 1)]
    listing = []
    for number in range(4):
        for k in range(tp_count):
            for x in range(2):

                def where(place, number=number, k=k, x=x):
                    tp = lax.rem(place[2] + (tp_count - k), tp_count)
                    row = tp * (2 * rows) + (place[1] ^ (number & 1)) * rows
                    col = (place[0] ^ (2 * x + (number >> 1))) * cols
                    return (row, col, k == 0)

                listing.append((number, (k, x), where))
    return Pieces(arrays, listing, (rows, cols), 2 * rows)


def fetch(copies, sems, base=0):
    started = [pltpu.make_async_copy(src, dst, sems.at[base + i]) for i, (src, dst) in enumerate(copies)]
    for copy in started:
        copy.start()
    return started


def group_mean(values, head_dim):
    width = values.shape[1]
    row = lax.broadcasted_iota(jnp.int32, (width, width), 0) // head_dim
    col = lax.broadcasted_iota(jnp.int32, (width, width), 1) // head_dim
    ones = jnp.where(row == col, 1.0 / head_dim, 0.0)
    return dot(values, ones, ((1,), (0,)), precision=lax.Precision.HIGHEST)


def half_turn(values, head_dim):
    width = values.shape[1]
    half = head_dim // 2
    lane = lax.broadcasted_iota(jnp.int32, values.shape, 1)
    low = (lane & (head_dim - 1)) < half
    return jnp.where(low, pltpu.roll(values, width - half, 1), pltpu.roll(values, half, 1)), low


def project_kernel(
    place, tok_ref, gain_ref, hgain_ref, cos_ref, sin_ref, w_in, normed_ref, raw_ref, q_ref, kv_ref,
    w_ref, sems, *, head_dim, q_cols, rot_cols, chunk,
):
    shard = w_in.shape[1]
    tile = tok_ref.shape[1]

    @pl.when(pl.program_id(0) == 0)
    def _():
        moves = []
        for m in range(w_in.shape[0]):
            row = pl.multiple_of((place[0] ^ m) * shard, shard)
            moves.append((w_in.at[m], w_ref.at[pl.ds(row, shard), :]))
        for copy in fetch(moves, sems):
            copy.wait()

    def norm(i, carry):
        rows = pl.ds(pl.multiple_of(i * chunk, chunk), chunk)
        x = tok_ref[0, rows, :].astype(F32)
        r = lax.rsqrt(jnp.mean(x * x, axis=-1, keepdims=True) + EPSILON)
        normed_ref[0, rows, :] = (x * r * gain_ref[...]).astype(BF16)
        return carry

    lax.fori_loop(0, tile // chunk, norm, 0)
    raw = mm(normed_ref[0], w_ref[...])
    raw_ref[0] = raw
    scale = lax.rsqrt(group_mean(raw * raw, head_dim) + EPSILON)
    n = raw * scale * hgain_ref[...]
    turned, low = half_turn(n, head_dim)
    rot = n * cos_ref[...] + jnp.where(low, -turned, turned) * sin_ref[...]
    lane = lax.broadcasted_iota(jnp.int32, raw.shape, 1)
    out = jnp.where(lane < rot_cols, rot, raw).astype(BF16)
    q_ref[0] = out[:, :q_cols]
    kv_ref[0] = out[:, q_cols:]


def project(place, tokens, gain, hgain, cos, sin, w_in, head_dim, q_cols, rot_cols):
    seqs, rows, width = tokens.shape
    cols = w_in.shape[2]
    row_spec = lambda last: pl.BlockSpec((1, rows, last), lambda s, *_: (s, 0, 0))
    flat = lambda shape: pl.BlockSpec(shape, lambda s, *_: (0,) * len(shape))
    return pl.pallas_call(
        functools.partial(
            project_kernel, head_dim=head_dim, q_cols=q_cols, rot_cols=rot_cols, chunk=64
        ),
        grid_spec=pltpu.PrefetchScalarGridSpec(
            num_scalar_prefetch=1,
            grid=(seqs,),
            in_specs=[
                row_spec(width), flat((1, width)), flat((1, cols)), flat((rows, cols)), flat((rows, cols)), ANY,
            ],
            out_specs=[row_spec(width), row_spec(cols), row_spec(q_cols), row_spec(cols - q_cols)],
            scratch_shapes=[
                pltpu.VMEM((width, cols), BF16), pltpu.SemaphoreType.DMA((w_in.shape[0],)),
            ],
        ),
        out_shape=[
            jax.ShapeDtypeStruct((seqs, rows, width), BF16),
            jax.ShapeDtypeStruct((seqs, rows, cols), F32),
            jax.ShapeDtypeStruct((seqs, rows, q_cols), BF16),
            jax.ShapeDtypeStruct((seqs, rows, cols - q_cols), BF16),
        ],
        compiler_params=params(),
        cost_estimate=cost(2 * seqs * rows * width * cols, seqs * rows * width * 4),
        name="project",
    )(place, tokens, gain, hgain, cos, sin, w_in)


def allowed_t(place, prefix, part, key_count, block, tile):
    j = lax.broadcasted_iota(jnp.int32, (key_count, tile), 0)
    key_pos = (place ^ (j // block)) * block + (j & (block - 1))
    query_pos = place * block + part * tile + lax.broadcasted_iota(jnp.int32, (key_count, tile), 1)
    return (key_pos <= query_pos) | (key_pos < prefix)


def attend_kernel(place, prefix, q_ref, kv_ref, out_ref, lse_ref, *, heads, head_dim, tile, block):
    seq = pl.program_id(0)
    part = pl.program_id(1)
    pairs = kv_ref[:, 0].reshape(-1, 2 * head_dim)
    keys = pairs[:, :head_dim]
    values = pairs[:, head_dim:]
    allowed = allowed_t(place[1], prefix[seq], part, pairs.shape[0], block, tile)
    for head in range(heads):
        lanes = slice(head * head_dim, (head + 1) * head_dim)
        scores = mm_t(keys, q_ref[0, :, lanes]) * (head_dim ** (-0.5))
        scores = jnp.where(allowed, scores, NEGATIVE)
        top = jnp.max(scores, axis=0, keepdims=True)
        weight = jnp.exp(scores - top)
        total = jnp.sum(weight, axis=0, keepdims=True)
        probs = weight * (1.0 / total)
        out_ref[0, :, lanes] = outer_sum(probs.astype(BF16), values).astype(BF16)
        lse_ref[0, head : head + 1, :] = top + jnp.log(total)


def attention_specs(seqs, rows, q_cols, heads, kv_all):
    tile = min(256, rows)
    blocks, _, block, pair = kv_all.shape
    row_block = pl.BlockSpec((1, tile, q_cols), lambda s, i, *_: (s, i, 0))
    key_block = pl.BlockSpec((blocks, 1, block, pair), lambda s, i, *_: (0, s, 0, 0))
    stat_block = pl.BlockSpec((1, heads, tile), lambda s, i, *_: (s, 0, i))
    return tile, blocks, block, pair, row_block, key_block, stat_block


def attend(place, prefix, query, kv_all, heads, head_dim):
    seqs, rows, q_cols = query.shape
    tile, blocks, block, pair, row_block, key_block, stat_block = attention_specs(
        seqs, rows, q_cols, heads, kv_all
    )
    elements = seqs * rows * blocks * block * heads
    return pl.pallas_call(
        functools.partial(attend_kernel, heads=heads, head_dim=head_dim, tile=tile, block=block),
        grid_spec=pltpu.PrefetchScalarGridSpec(
            num_scalar_prefetch=2,
            grid=(seqs, rows // tile),
            in_specs=[row_block, key_block],
            out_specs=[row_block, stat_block],
        ),
        out_shape=[
            jax.ShapeDtypeStruct((seqs, rows, q_cols), BF16),
            jax.ShapeDtypeStruct((seqs, heads, rows), F32),
        ],
        compiler_params=params(),
        cost_estimate=cost(elements * 1024, query.size * 4, elements),
        name="attend",
    )(place, prefix, query, kv_all)


def attend_back_kernel(
    place, prefix, q_ref, kv_ref, d_ref, lse_ref, dq_ref, dkv_ref, *, heads, head_dim, tile, block
):
    seq = pl.program_id(0)
    part = pl.program_id(1)
    scale = head_dim ** (-0.5)
    pairs = kv_ref[:, 0].reshape(-1, 2 * head_dim)
    keys = pairs[:, :head_dim]
    values = pairs[:, head_dim:]
    allowed = allowed_t(place[1], prefix[seq], part, pairs.shape[0], block, tile)
    dkeys = None
    dvalues = None
    for head in range(heads):
        lanes = slice(head * head_dim, (head + 1) * head_dim)
        query = q_ref[0, :, lanes]
        dout = d_ref[0, :, lanes]
        scores = mm_t(keys, query) * scale
        probs = jnp.where(allowed, jnp.exp(scores - lse_ref[0, head : head + 1, :]), 0.0)
        weighted = probs * mm_t(values, dout)
        delta = jnp.sum(weighted, axis=0, keepdims=True)
        dscore = (weighted - probs * delta).astype(BF16)
        dv = mm(probs.astype(BF16), dout)
        dk = mm(dscore, query)
        dkeys = dk if dkeys is None else dkeys + dk
        dvalues = dv if dvalues is None else dvalues + dv
        dq_ref[0, :, lanes] = outer_sum(dscore, keys) * scale
    both = jnp.concatenate([dkeys * scale, dvalues], axis=1).reshape(dkv_ref.shape[0], block, -1)

    @pl.when(part == 0)
    def _():
        dkv_ref[:, 0] = both

    @pl.when(part > 0)
    def _():
        dkv_ref[:, 0] += both


def attend_back(place, prefix, query, kv_all, dout, lse, heads, head_dim):
    seqs, rows, q_cols = query.shape
    tile, blocks, block, pair, row_block, key_block, stat_block = attention_specs(
        seqs, rows, q_cols, heads, kv_all
    )
    elements = seqs * rows * blocks * block * heads
    return pl.pallas_call(
        functools.partial(attend_back_kernel, heads=heads, head_dim=head_dim, tile=tile, block=block),
        grid_spec=pltpu.PrefetchScalarGridSpec(
            num_scalar_prefetch=2,
            grid=(seqs, rows // tile),
            in_specs=[row_block, key_block, row_block, stat_block],
            out_specs=[row_block, key_block],
        ),
        out_shape=[
            jax.ShapeDtypeStruct((seqs, rows, q_cols), F32),
            jax.ShapeDtypeStruct((blocks, seqs, block, pair), F32),
        ],
        compiler_params=params(),
        cost_estimate=cost(elements * 2560, query.size * 8, elements),
        name="attend_back",
    )(place, prefix, query, kv_all, dout, lse)


def residual_kernel(*refs, tp_count, out_w, down_w, step):
    place, tok_ref, og_ref, gain_ref = refs[:4]
    refs = refs[4:]
    att_in, refs = refs[:tp_count], refs[tp_count:]
    out_in, refs = refs[: len(out_w.arrays)], refs[len(out_w.arrays) :]
    down_in, refs = refs[: len(down_w.arrays)], refs[len(down_w.arrays) :]
    res_ref, fin_ref, dh_ref, att, wo, wd, sems = refs
    seq = pl.program_id(0)
    tile = tok_ref.shape[1]
    width = tok_ref.shape[2]
    cols = att_in[0].shape[1]

    @pl.when(seq == 0)
    def _():
        moves = []
        for k in range(tp_count):
            col = lax.rem(place[2] + (tp_count - k), tp_count) * cols
            moves.append((att_in[k], att.at[:, pl.ds(pl.multiple_of(col, cols), cols)]))
        moves += list(out_w.copies(place, out_in, wo))
        first = fetch(moves, sems)
        second = fetch(list(down_w.copies(place, down_in, wd)), sems, len(first))
        for copy in first + second:
            copy.wait()

    base = pl.multiple_of(seq * tile, tile)

    def out_part(i, total):
        lanes = pl.ds(pl.multiple_of(i * step, step), step)
        res = tok_ref[0, :, lanes].astype(F32) + mm(att[pl.ds(base, tile), :], wo[:, lanes])
        res_ref[0, :, lanes] = res
        return total + res * res

    total = lax.fori_loop(0, width // step, out_part, jnp.zeros((tile, step), F32))
    r = lax.rsqrt(jnp.sum(total, axis=-1, keepdims=True) / width + EPSILON)

    def norm(i, carry):
        lanes = pl.ds(pl.multiple_of(i * step, step), step)
        fin_ref[0, :, lanes] = (res_ref[0, :, lanes] * r * gain_ref[:, lanes]).astype(BF16)
        return carry

    lax.fori_loop(0, width // step, norm, 0)

    def back(i, carry):
        part = pl.ds(pl.multiple_of(i * step, step), step)
        dh_ref[0, :, part] = mm_t(og_ref[0], wd[part, :])
        return carry

    lax.fori_loop(0, wd.shape[0] // step, back, 0)


def residual_part(place, tokens, out_grad, gain, att, out_w, down_w, hidden_cols):
    seqs, rows, width = tokens.shape
    inner = att[0].shape[1] * len(att)
    row_spec = lambda last: pl.BlockSpec((1, rows, last), lambda s, *_: (s, 0, 0))
    count = len(att) + len(out_w.listing) + len(down_w.listing)
    arrays = list(att) + out_w.arrays + down_w.arrays
    return pl.pallas_call(
        functools.partial(residual_kernel, tp_count=len(att), out_w=out_w, down_w=down_w, step=256),
        grid_spec=pltpu.PrefetchScalarGridSpec(
            num_scalar_prefetch=1,
            grid=(seqs,),
            in_specs=[row_spec(width), row_spec(width), pl.BlockSpec((1, width), lambda s, *_: (0, 0))]
            + [ANY] * len(arrays),
            out_specs=[row_spec(width), row_spec(width), row_spec(hidden_cols)],
            scratch_shapes=[
                pltpu.VMEM((seqs * rows, inner), BF16),
                pltpu.VMEM((inner, width), BF16),
                pltpu.VMEM((hidden_cols, width), BF16),
                pltpu.SemaphoreType.DMA((count,)),
            ],
        ),
        out_shape=[
            jax.ShapeDtypeStruct((seqs, rows, width), F32),
            jax.ShapeDtypeStruct((seqs, rows, width), BF16),
            jax.ShapeDtypeStruct((seqs, rows, hidden_cols), F32),
        ],
        compiler_params=params(),
        cost_estimate=cost(2 * seqs * rows * width * (inner + hidden_cols), seqs * rows * width * 12),
        name="residual_part",
    )(place, tokens, out_grad, gain, *arrays)


def ffn_kernel(*refs, gate_w, up_w, down_w, out_w, step, chunk, own_cols):
    place, res_ref, fin_ref, dh_ref, og_ref, gain_ref = refs[:6]
    refs = refs[6:]
    gate_in, refs = refs[: len(gate_w.arrays)], refs[len(gate_w.arrays) :]
    down_in, refs = refs[: len(down_w.arrays)], refs[len(down_w.arrays) :]
    out_in, refs = refs[: len(out_w.arrays)], refs[len(out_w.arrays) :]
    (
        lay_ref, dres_ref, hid_ref, dgate_ref, dup_ref, datt_ref, gsum_ref,
        wg, wu, wd, wo, hid, dgate, dup, lift, sems,
    ) = refs
    seq = pl.program_id(0)
    tile = res_ref.shape[1]
    width = res_ref.shape[2]
    ff = wd.shape[0]

    @pl.when(seq == 0)
    def _():
        moves = list(gate_w.copies(place, gate_in, wg)) + list(up_w.copies(place, gate_in, wu))
        moves += list(down_w.copies(place, down_in, wd)) + list(out_w.copies(place, out_in, wo, True))
        for copy in fetch(moves, sems):
            copy.wait()

    def square(i, total):
        lanes = pl.ds(pl.multiple_of(i * step, step), step)
        res = res_ref[0, :, lanes]
        return total + res * res

    total = lax.fori_loop(0, width // step, square, jnp.zeros((tile, step), F32))
    r = lax.rsqrt(jnp.sum(total, axis=-1, keepdims=True) / width + EPSILON)

    def inner(i, carry):
        lanes = pl.ds(pl.multiple_of(i * step, step), step)
        gate = mm(fin_ref[0], wg[:, lanes])
        up = mm(fin_ref[0], wu[:, lanes])
        grad = dh_ref[0, :, lanes]
        sig = 1.0 / (1.0 + jnp.exp(-gate))
        silu = gate * sig
        hid[:, lanes] = (silu * up).astype(BF16)
        dgate[:, lanes] = (grad * up * sig * (1.0 + gate * (1.0 - sig))).astype(BF16)
        dup[:, lanes] = (grad * silu).astype(BF16)
        return carry

    lax.fori_loop(0, ff // step, inner, 0)
    own = pl.ds(pl.multiple_of(place[2] * own_cols, own_cols), own_cols)
    hid_ref[0] = hid[:, own]
    dgate_ref[0] = dgate[:, own]
    dup_ref[0] = dup[:, own]

    def outer(i, total):
        lanes = pl.ds(pl.multiple_of(i * step, step), step)
        res = res_ref[0, :, lanes]
        lay_ref[0, :, lanes] = (res + mm(hid[...], wd[:, lanes])).astype(BF16)
        grad = mm_t(dgate[...], wg[lanes, :]) + mm_t(dup[...], wu[lanes, :])
        gsum = jnp.sum(grad * res * r, axis=0, keepdims=True)

        @pl.when(seq == 0)
        def _():
            gsum_ref[:, lanes] = gsum

        @pl.when(seq > 0)
        def _():
            gsum_ref[:, lanes] += gsum

        u = grad * gain_ref[:, lanes]
        lift[:, lanes] = u
        return total + res * u

    total = lax.fori_loop(0, width // step, outer, jnp.zeros((tile, step), F32))
    pull = r * r * r * (jnp.sum(total, axis=-1, keepdims=True) / width)

    def finish(i, carry):
        lanes = pl.ds(pl.multiple_of(i * step, step), step)
        grad = og_ref[0, :, lanes].astype(F32) + r * lift[:, lanes] - res_ref[0, :, lanes] * pull
        dres_ref[0, :, lanes] = grad.astype(BF16)
        return carry

    lax.fori_loop(0, width // step, finish, 0)
    datt_ref[0] = mm_t(dres_ref[0], wo[...]).astype(BF16)


def ffn(place, residual, ffn_in, dhidden, out_grad, gain, gate_w, up_w, down_w, out_w, own_cols, q_cols):
    seqs, rows, width = residual.shape
    hidden_cols = dhidden.shape[2]
    row_spec = lambda last: pl.BlockSpec((1, rows, last), lambda s, *_: (s, 0, 0))
    vec = pl.BlockSpec((1, width), lambda s, *_: (0, 0))
    arrays = gate_w.arrays + down_w.arrays + out_w.arrays
    count = len(gate_w.listing) * 2 + len(down_w.listing) + len(out_w.listing)
    once = dict(pipeline_mode=pl.Buffered(1))
    row_once = lambda last: pl.BlockSpec((1, rows, last), lambda s, *_: (s, 0, 0), **once)
    return pl.pallas_call(
        functools.partial(
            ffn_kernel, gate_w=gate_w, up_w=up_w, down_w=down_w, out_w=out_w, step=256, chunk=64,
            own_cols=own_cols,
        ),
        grid_spec=pltpu.PrefetchScalarGridSpec(
            num_scalar_prefetch=1,
            grid=(seqs,),
            in_specs=[row_spec(width), row_spec(width), row_spec(hidden_cols), row_spec(width), vec]
            + [ANY] * len(arrays),
            out_specs=[
                row_spec(width), row_spec(width), row_spec(own_cols), row_spec(own_cols), row_spec(own_cols),
                row_spec(q_cols), vec,
            ],
            scratch_shapes=[
                pltpu.VMEM((width, hidden_cols), BF16),
                pltpu.VMEM((width, hidden_cols), BF16),
                pltpu.VMEM((hidden_cols, width), BF16),
                pltpu.VMEM((q_cols, width), BF16),
                pltpu.VMEM((rows, hidden_cols), BF16),
                pltpu.VMEM((rows, hidden_cols), BF16),
                pltpu.VMEM((rows, hidden_cols), BF16),
                pltpu.VMEM((rows, width), F32),
                pltpu.SemaphoreType.DMA((count,)),
            ],
        ),
        out_shape=[
            jax.ShapeDtypeStruct((seqs, rows, width), BF16),
            jax.ShapeDtypeStruct((seqs, rows, width), BF16),
            jax.ShapeDtypeStruct((seqs, rows, own_cols), BF16),
            jax.ShapeDtypeStruct((seqs, rows, own_cols), BF16),
            jax.ShapeDtypeStruct((seqs, rows, own_cols), BF16),
            jax.ShapeDtypeStruct((seqs, rows, q_cols), BF16),
            jax.ShapeDtypeStruct((1, width), F32),
        ],
        compiler_params=params(),
        cost_estimate=cost(
            2 * seqs * rows * width * (5 * hidden_cols + q_cols), seqs * rows * width * 14
        ),
        name="ffn",
    )(place, residual, ffn_in, dhidden, out_grad, gain, *arrays)


def head_back_kernel(
    raw_ref, dq_ref, dkv_ref, hgain_ref, cos_ref, sin_ref, out_ref, gsum_ref, *, head_dim, rot_cols
):
    seq = pl.program_id(0)
    raw = raw_ref[0]
    grad = jnp.concatenate([dq_ref[0], dkv_ref[0]], axis=1)
    lane = lax.broadcasted_iota(jnp.int32, raw.shape, 1)
    turned, low = half_turn(grad * sin_ref[...], head_dim)
    dn = grad * cos_ref[...] + jnp.where(low, turned, -turned)
    r = lax.rsqrt(group_mean(raw * raw, head_dim) + EPSILON)
    u = dn * hgain_ref[...]
    mean = group_mean(raw * u, head_dim)
    draw = r * u - raw * (r * r * r * mean)
    out_ref[0] = jnp.where(lane < rot_cols, draw, grad).astype(BF16)
    gsum = jnp.sum(dn * raw * r, axis=0, keepdims=True)

    @pl.when(seq == 0)
    def _():
        gsum_ref[...] = gsum

    @pl.when(seq > 0)
    def _():
        gsum_ref[...] += gsum


def head_back(raw, dq, dkv, hgain, cos, sin, head_dim, rot_cols):
    seqs, rows, cols = raw.shape
    row_spec = lambda last: pl.BlockSpec((1, rows, last), lambda s: (s, 0, 0))
    flat = lambda shape: pl.BlockSpec(shape, lambda s: (0, 0))
    return pl.pallas_call(
        functools.partial(head_back_kernel, head_dim=head_dim, rot_cols=rot_cols),
        grid=(seqs,),
        in_specs=[
            row_spec(cols), row_spec(dq.shape[2]), row_spec(dkv.shape[2]), flat((1, cols)),
            flat((rows, cols)), flat((rows, cols)),
        ],
        out_specs=[row_spec(cols), flat((1, cols))],
        out_shape=[
            jax.ShapeDtypeStruct((seqs, rows, cols), BF16),
            jax.ShapeDtypeStruct((1, cols), F32),
        ],
        compiler_params=params(),
        cost_estimate=cost(seqs * rows * cols * cols * 8, seqs * rows * cols * 14),
        name="head_back",
    )(raw, dq, dkv, hgain, cos, sin)


def input_kernel(*refs, tp_count, qkv_w, step, chunk):
    place, tok_ref, dres_ref, gain_ref = refs[:4]
    refs = refs[4:]
    d_in, refs = refs[:tp_count], refs[tp_count:]
    w_in, refs = refs[: len(qkv_w.arrays)], refs[len(qkv_w.arrays) :]
    out_ref, gsum_ref, dall, w, lift, sems = refs
    seq = pl.program_id(0)
    tile = tok_ref.shape[1]
    width = tok_ref.shape[2]
    cols = d_in[0].shape[1]

    @pl.when(seq == 0)
    def _():
        moves = []
        for k in range(tp_count):
            col = lax.rem(place[2] + (tp_count - k), tp_count) * cols
            moves.append((d_in[k], dall.at[:, pl.ds(pl.multiple_of(col, cols), cols)]))
        moves += list(qkv_w.copies(place, w_in, w))
        for copy in fetch(moves, sems):
            copy.wait()

    base = pl.multiple_of(seq * tile, tile)

    def square(i, total):
        lanes = pl.ds(pl.multiple_of(i * step, step), step)
        x = tok_ref[0, :, lanes].astype(F32)
        return total + x * x

    total = lax.fori_loop(0, width // step, square, jnp.zeros((tile, step), F32))
    r = lax.rsqrt(jnp.sum(total, axis=-1, keepdims=True) / width + EPSILON)

    def outer(i, total):
        lanes = pl.ds(pl.multiple_of(i * step, step), step)
        x = tok_ref[0, :, lanes].astype(F32)
        grad = mm_t(dall[pl.ds(base, tile), :], w[lanes, :])
        gsum = jnp.sum(grad * x * r, axis=0, keepdims=True)

        @pl.when(seq == 0)
        def _():
            gsum_ref[:, lanes] = gsum

        @pl.when(seq > 0)
        def _():
            gsum_ref[:, lanes] += gsum

        u = grad * gain_ref[:, lanes]
        lift[:, lanes] = u
        return total + x * u

    total = lax.fori_loop(0, width // step, outer, jnp.zeros((tile, step), F32))
    pull = r * r * r * (jnp.sum(total, axis=-1, keepdims=True) / width)

    def finish(i, carry):
        lanes = pl.ds(pl.multiple_of(i * step, step), step)
        x = tok_ref[0, :, lanes].astype(F32)
        grad = dres_ref[0, :, lanes].astype(F32) + r * lift[:, lanes] - x * pull
        out_ref[0, :, lanes] = grad.astype(BF16)
        return carry

    lax.fori_loop(0, width // step, finish, 0)


def input_part(place, tokens, dres, gain, pieces, qkv_w):
    seqs, rows, width = tokens.shape
    inner = pieces[0].shape[1] * len(pieces)
    row_spec = lambda last: pl.BlockSpec((1, rows, last), lambda s, *_: (s, 0, 0))
    vec = pl.BlockSpec((1, width), lambda s, *_: (0, 0))
    arrays = list(pieces) + qkv_w.arrays
    return pl.pallas_call(
        functools.partial(input_kernel, tp_count=len(pieces), qkv_w=qkv_w, step=256, chunk=64),
        grid_spec=pltpu.PrefetchScalarGridSpec(
            num_scalar_prefetch=1,
            grid=(seqs,),
            in_specs=[row_spec(width), row_spec(width), vec] + [ANY] * len(arrays),
            out_specs=[row_spec(width), vec],
            scratch_shapes=[
                pltpu.VMEM((seqs * rows, inner), BF16),
                pltpu.VMEM((width, inner), BF16),
                pltpu.VMEM((rows, width), F32),
                pltpu.SemaphoreType.DMA((len(pieces) + len(qkv_w.listing),)),
            ],
        ),
        out_shape=[
            jax.ShapeDtypeStruct((seqs, rows, width), BF16),
            jax.ShapeDtypeStruct((1, width), F32),
        ],
        compiler_params=params(),
        cost_estimate=cost(2 * seqs * rows * width * inner, seqs * rows * width * 6),
        name="input_part",
    )(place, tokens, dres, gain, *arrays)


def weight_grad_kernel(place, *refs, count):
    keep_ref, give_ref = refs[-2:]
    step = pl.program_id(0)
    for i in range(count):
        grad = outer_sum(refs[2 * i][...], refs[2 * i + 1][...])

        @pl.when(step < 2)
        def _():
            keep_ref[0, i] = grad

        @pl.when(step >= 2)
        def _():
            give_ref[0, i] = grad.astype(BF16)


def weight_grad(place, pairs, cut_left, name):
    rows = pairs[0][0].shape[0]
    left_cols, right_cols = pairs[0][0].shape[1], pairs[0][1].shape[1]

    def piece(step, place):
        return place[0] ^ (2 * (step & 1) + (step >> 1))

    moving = lambda cols: pl.BlockSpec((rows, cols // 4), lambda m, place: (0, piece(m, place)))
    fixed = lambda cols: pl.BlockSpec((rows, cols), lambda m, place: (0, 0))
    if cut_left:
        specs = [moving(left_cols), fixed(right_cols)]
        shape = (left_cols // 4, right_cols)
    else:
        specs = [fixed(left_cols), moving(right_cols)]
        shape = (left_cols, right_cols // 4)
    count = len(pairs)
    block = (1, count) + shape
    return pl.pallas_call(
        functools.partial(weight_grad_kernel, count=count),
        grid_spec=pltpu.PrefetchScalarGridSpec(
            num_scalar_prefetch=1,
            grid=(4,),
            in_specs=specs * count,
            out_specs=[
                pl.BlockSpec(block, lambda m, place: (jnp.minimum(m, 1), 0, 0, 0)),
                pl.BlockSpec(block, lambda m, place: (jnp.maximum(m - 2, 0), 0, 0, 0)),
            ],
        ),
        out_shape=[
            jax.ShapeDtypeStruct((2,) + block[1:], F32),
            jax.ShapeDtypeStruct((2,) + block[1:], BF16),
        ],
        compiler_params=params(),
        cost_estimate=cost(2 * count * rows * left_cols * right_cols, count * rows * (left_cols + right_cols) * 2),
        name=name,
    )(place, *[array for pair in pairs for array in pair])


def settle(keep, give):
    total = keep + swap(give, "fsdp", 1).astype(F32)
    total = total[0] + swap(total[1].astype(BF16), "fsdp", 2).astype(F32)
    return cube_sum(total, "ctx")


def shards(
    tokens, attn_gain, w_query, key_matrix, value_matrix, query_gain, key_gain, w_out, ffn_gain,
    w_gate, w_up, w_down, prefix_len, out_grad,
):
    seqs, block_len, width = tokens.shape
    rows = seqs * block_len
    place = place_of()
    ctx_count = lax.axis_size("ctx")
    fsdp_count = lax.axis_size("fsdp")
    tp_count = lax.axis_size("tp")
    head_dim = query_gain.shape[0] * fsdp_count
    q_cols = w_query.shape[1]
    kv_cols = key_matrix.shape[1]
    heads = q_cols // head_dim
    own_ff = w_gate.shape[1]
    hidden_cols = own_ff * tp_count
    rot_cols = q_cols + kv_cols

    gains = lax.all_gather(
        jnp.concatenate([attn_gain, ffn_gain, query_gain, key_gain]), "fsdp", axis=0
    ).astype(F32)
    a, q = attn_gain.size, query_gain.size
    attn_gain32 = gains[:, :a].reshape(1, -1)
    ffn_gain32 = gains[:, a : 2 * a].reshape(1, -1)
    query_gain32 = gains[:, 2 * a : 2 * a + q].reshape(1, -1)
    key_gain32 = gains[:, 2 * a + q :].reshape(1, -1)
    hgain = jnp.concatenate(
        [query_gain32] * heads + [key_gain32] * (kv_cols // head_dim) + [jnp.ones((1, kv_cols), F32)], axis=1
    )
    query_pos = place[1] * block_len + jnp.arange(block_len, dtype=jnp.int32)
    cos_half, sin_half = rotary_tables(query_pos, head_dim)
    copies = 2 * (rot_cols + kv_cols) // head_dim
    cos = jnp.concatenate([cos_half] * copies, axis=1)
    sin = jnp.concatenate([sin_half] * copies, axis=1)

    w_qkv = jnp.concatenate([w_query, key_matrix, value_matrix], axis=1)
    near = jnp.stack([w_qkv, swap(w_qkv, "fsdp", 2)])
    far = swap(near, "fsdp", 1)
    own_qkv = jnp.stack([near[0], far[0], near[1], far[1]])

    gate_up = lax.all_gather(jnp.stack([w_gate, w_up]), ("fsdp", "tp"), axis=0)
    gate_w = gathered_columns(gate_up, (0,), fsdp_count, tp_count, w_gate.shape)
    up_w = gathered_columns(gate_up, (1,), fsdp_count, tp_count, w_up.shape)
    if ctx_count == 2:
        w_out_late = after(w_out, near)
        out_w = travelled_rows(w_out_late, tp_count)
        down_w = travelled_rows(after(w_down, out_w.arrays[0]), tp_count)
    else:
        out_down = lax.all_gather(jnp.stack([w_out, w_down]), ("fsdp", "tp"), axis=0)
        out_w = gathered_rows(out_down, (0,), fsdp_count, tp_count, w_out.shape)
        down_w = gathered_rows(out_down, (1,), fsdp_count, tp_count, w_down.shape)
    qkv_late = after(w_qkv, gate_up)
    qkv_all = lax.all_gather(qkv_late, ("fsdp", "tp"), axis=0)
    qkv_w = gathered_columns(qkv_all, (), fsdp_count, tp_count, w_qkv.shape)

    normed, raw, query_low, kv_low = project(
        place, tokens, attn_gain32, hgain, cos, sin, own_qkv, head_dim, q_cols, rot_cols
    )
    kv_all = cube(kv_low, "ctx")
    attended, lse = attend(place, prefix_len, query_low, kv_all, heads, head_dim)
    attended = attended.reshape(rows, q_cols)
    att = ring(attended, "tp")
    residual, ffn_in, dhidden = residual_part(
        place, tokens, out_grad, ffn_gain32, att, out_w, down_w, hidden_cols
    )
    if ctx_count == 2:
        own_out_w = out_w
    else:
        own_out = lax.all_gather(w_out, "fsdp", axis=0)
        own_out_w = Pieces(
            [own_out],
            [(0, (f,), lambda p, f=f: (p[2] * w_out.shape[0], f * w_out.shape[1], True)) for f in range(fsdp_count)],
            w_out.shape,
            w_out.shape[0],
        )
    layer_low, dres_low, hidden, dgate, dup, dattended, gsum_ffn = ffn(
        place, residual, ffn_in, dhidden, out_grad, ffn_gain32, gate_w, up_w, down_w, own_out_w, own_ff, q_cols
    )
    dquery, dkv = attend_back(place, prefix_len, query_low, kv_all, dattended, lse, heads, head_dim)
    flat = lambda value: value.reshape(rows, -1)
    down_out = weight_grad(
        place, [(flat(hidden), flat(out_grad)), (attended, flat(dres_low))], False, "grad_down_out"
    )
    gate_up_grad = weight_grad(
        place, [(flat(ffn_in), flat(dgate)), (flat(ffn_in), flat(dup))], True, "grad_gate_up"
    )
    owned = cube_own(dkv, "ctx")
    dqkv, gsum_head = head_back(raw, dquery, owned, hgain, cos, sin, head_dim, rot_cols)
    dqkv = flat(dqkv)
    pieces = ring(dqkv, "tp")
    qkv_grad = weight_grad(place, [(flat(normed), dqkv)], True, "grad_qkv")
    input_grad, gsum_attn = input_part(place, tokens, dres_low, attn_gain32, pieces, qkv_w)

    down_out = settle(*down_out)
    gate_up_grad = settle(*gate_up_grad)
    qkv_grad = settle(*qkv_grad)[0]
    head_sum = gsum_head.reshape(-1, head_dim)
    query_sum = jnp.sum(head_sum[:heads], axis=0)
    key_sum = jnp.sum(head_sum[heads : heads + kv_cols // head_dim], axis=0)
    head_gains = jnp.concatenate([query_sum, key_sum])[None]
    head_gains = lax.psum(head_gains, "tp")[0]
    gain_grads = jnp.concatenate([gsum_attn[0], gsum_ffn[0], head_gains])
    gain_grads = cube_sum(cube_sum(gain_grads, "fsdp"), "ctx")
    member = lax.axis_index("fsdp")

    def share(low, high):
        size = (high - low) // fsdp_count
        return lax.dynamic_slice_in_dim(gain_grads[low:high], member * size, size, 0)

    ends = [0, width, 2 * width, 2 * width + head_dim, 2 * width + 2 * head_dim]
    return (
        layer_low,
        input_grad,
        share(ends[0], ends[1]),
        qkv_grad[:, :q_cols],
        qkv_grad[:, q_cols : q_cols + kv_cols],
        qkv_grad[:, q_cols + kv_cols :],
        share(ends[2], ends[3]),
        share(ends[3], ends[4]),
        down_out[1],
        share(ends[1], ends[2]),
        gate_up_grad[0],
        gate_up_grad[1],
        down_out[0],
    )


def solution(mesh):
    columns = P("fsdp", "tp")
    across = P("tp", "fsdp")
    vector = P("fsdp")
    data = P("fsdp", "ctx", None)
    return jax.shard_map(
        shards,
        mesh=mesh,
        in_specs=(
            data, vector, columns, columns, columns, vector, vector, across, vector,
            columns, columns, across, vector, data,
        ),
        out_specs=(
            data, data, vector, columns, columns, columns, vector, vector, across, vector,
            columns, columns, across,
        ),
        check_vma=False,
    )
```

time: 547 us -> 453 us (0.83); the launches traced: 539 us -> 452 us
  Pallas kernels: 31.1 us -> 187 us
  local copies, waits for them, and re-layouts: 122 us -> 19 us
  matrix products: 93 us -> 0 us
  other arithmetic: 55.3 us -> 14.1 us
  between operations: 2.82 us -> 15.2 us
  blocking collectives: 34.8 us -> 27.8 us
  starting transfers between devices: 37.2 us -> 30.4 us
    pallas_call x0 -> x8, Pallas kernels: none -> 153 us  [the longest x1 51.6 us: ffn(): pl.pallas_call(functools.partial(ffn_kernel, gate_w=gate_w, up_w=up_w, do...]
    dot_general x15 -> x0, matrix products: 93 us -> none  [dot(): lax.dot_general(left, right, (dims, ((), ())), preferred_element_type=F32)]
    dynamic_update_slice x55 -> x0, local copies, waits for them, and re-layouts: 51.1 us -> none  [the longest x29 28.1 us: cube_gather(): lax.dynamic_update_slice_in_dim(whole, piece, (me ^ mask) * width, dim)]
    ppermute x59 -> x36, waiting for transfers between devices: 162 us -> 138 us  [the longest x12 73.6 us: ring(): lax.ppermute(pieces[-1], axis, [(i, (i + 1) % size) for i in range(size)])]
    convert_element_type x9 -> x0, other arithmetic: 22.5 us -> none  [the longest x1 10.3 us: shards(): input_grad = (dresidual + dinput).astype(BF16)]
    all_gather x0 -> x2, waiting for transfers between devices: none -> 20.6 us  [the longest x1 20.6 us: shards(): gate_up = lax.all_gather(jnp.stack([w_gate, w_up]), ('fsdp', 'tp'), axis=0)]
    dot_general x3 -> x0, local copies, waits for them, and re-layouts: 19.3 us -> none  [dot(): lax.dot_general(left, right, (dims, ((), ())), preferred_element_type=F32)]
    psum x2 -> x1, blocking collectives: 34.8 us -> 16.1 us  [shards(): head_gains = lax.psum(head_gains, 'tp')[0]]
  transfers between devices with their start and end apart: 59 -> 38, of which waited for: 24 -> 20; matrix products, arithmetic and copies ran while one was open for 44% -> 6% of each run, Pallas kernels for 6% -> 41%
where the time goes in v2:
time: 453 us; the launch traced here: 452 us
  Pallas kernels  187 us (41%)
  waiting for transfers between devices  158 us (35%)
  starting transfers between devices  30.4 us (7%)
  blocking collectives  27.8 us (6%)
  local copies, waits for them, and re-layouts  19 us (4%)
  between operations  15.2 us (3%)
  other arithmetic  14.1 us (3%)
    ppermute x12, waiting for transfers between devices, ring(): lax.ppermute(pieces[-1], axis, [(i, (i + 1) % size) for i in range(size)])  73.6 us
    ppermute x24, waiting for transfers between devices, swap(): lax.ppermute(value, axis, [(i, i ^ bit) for i in range(lax.axis_size(axis...  64 us
    pallas_call x1, Pallas kernels, ffn(): pl.pallas_call(functools.partial(ffn_kernel, gate_w=gate_w, up_w=up_w, do...  51.6 us
    pallas_call x1, Pallas kernels, residual_part(): pl.pallas_call(functools.partial(residual_kernel, tp_count=len(att), out_...  26.2 us
    pallas_call x3, Pallas kernels, weight_grad(): pl.pallas_call(functools.partial(weight_grad_kernel, count=count), grid_s...  26.1 us
    pallas_call x1, Pallas kernels, input_part(): pl.pallas_call(functools.partial(input_kernel, tp_count=len(pieces), qkv_...  25.7 us
    ppermute x24, starting transfers between devices, swap(): lax.ppermute(value, axis, [(i, i ^ bit) for i in range(lax.axis_size(axis...  22.4 us
    all_gather x1, waiting for transfers between devices, shards(): gate_up = lax.all_gather(jnp.stack([w_gate, w_up]), ('fsdp', 'tp'), axis=0)  20.6 us
  transfers between devices with their start and end apart: 38, of which 20 were waited for; matrix products, arithmetic and copies ran while one was open for 6% of the time, Pallas kernels for 41%

profile of v2, /device:TPU:0, one launch (start us, length us, event | category | flops | bytes accessed | tf_op | source)
XLA Modules:
  0.0 451.7 jit_solution(8050370504108335996)
XLA Ops:
  14.5 9.5 %collective-permute-done = bf16[512,384]{1,0:T(8,128)(2,1)S(1)} collective-permute-done((bf16[512,384]{1,0:T(8,128)(2,1)S(1)}, bf16[512,384]{1,0:T(8,128)(2,1)S(1)}, u32[]{:S(2)}, u32[]{:S(2)}) %collective-permute-start) | collective-permute-done | bytes 393248 | tf_op jit(solution)/shard_map/ppermute | solution.py:52
  27.5 5.2 %collective-permute-done.6 = bf16[128,512]{1,0:T(8,128)(2,1)S(1)} collective-permute-done((bf16[128,512]{1,0:T(8,128)(2,1)S(1)}, bf16[128,512]{1,0:T(8,128)(2,1)S(1)}, u32[]{:S(2)}, u32[]{:S(2)}) %collective-permute-start.6) | collective-permute-done | bytes 131104 | tf_op jit(solution)/shard_map/ppermute | solution.py:52
  34.3 14.1 %collective-permute-done.7 = bf16[2,128,512]{2,1,0:T(8,128)(2,1)S(1)} collective-permute-done((bf16[2,128,512]{2,1,0:T(8,128)(2,1)S(1)}, bf16[2,128,512]{2,1,0:T(8,128)(2,1)S(1)}, u32[]{:S(2)}, u32[]{:S(2)}) %collective-permute-start.7) | collective-permute-done | bytes 262176 | tf_op jit(solution)/shard_map/ppermute | solution.py:63
  48.5 8.4 %collective-permute-done.8 = bf16[2,128,512]{2,1,0:T(8,128)(2,1)S(1)} collective-permute-done((bf16[2,128,512]{2,1,0:T(8,128)(2,1)S(1)}, bf16[2,128,512]{2,1,0:T(8,128)(2,1)S(1)}, u32[]{:S(2)}, u32[]{:S(2)}) %collective-permute-start.8) | collective-permute-done | bytes 262176 | tf_op jit(solution)/shard_map/ppermute | solution.py:63
  58.4 11.8 %all-reduce = bf16[4224]{0:T(1024)(128)(2,1)S(1)} all-reduce(bf16[4224]{0:T(1024)(128)(2,1)S(1)} %dynamic-update-slice), channel_id=2, replica_groups=mesh['fsdp'=4,'ctx'=2,'tp'=4] {'fsdp'}, use_global_device_ids=true, to_apply=%add | all-reduce | flops 4224 | bytes 16896
  82.9 20.6 %all-gather.6.cloned.1.call-done = bf16[32,512,256]{2,1,0:T(8,128)(2,1)} async-done(((bf16[2,512,256]{2,1,0:T(8,128)(2,1)}), bf16[32,512,256]{2,1,0:T(8,128)(2,1)}) %all-gather.6.cloned.1.call-update) | async-done | bytes 8388624 | tf_op jit(solution)/shard_map/all_gather | solution.py:830
  111.7 10.4 %collective-permute-done.15 = bf16[2,128,512]{2,1,0:T(8,128)(2,1)S(1)} collective-permute-done((bf16[2,128,512]{2,1,0:T(8,128)(2,1)S(1)}, bf16[2,128,512]{2,1,0:T(8,128)(2,1)S(1)}, u32[]{:S(2)}, u32[]{:S(2)}) %collective-permute-start.15) | collective-permute-done | bytes 262176 | tf_op jit(solution)/shard_map/ppermute | solution.py:63
  122.1 14.3 %project.1 = (bf16[2,512,2048]{2,1,0:T(8,128)(2,1)}, f32[2,512,384]{2,1,0:T(8,128)}, bf16[2,512,256]{2,1,0:T(8,128)(2,1)}, bf16[2,512,128]{2,1,0:T(8,128)(2,1)}) custom-call(s32[3]{0:T(128)} %pad_add_fusion.place.refs_0_, bf16[2,512,2048]{2,1,0:T(8,128)(2,1)} %refs_1_.3, f32[1,2048]{1,0:T(1,128)} %bitcast.112, f32[1,384]{1,0:T(1,128)} %concatenate.26.hgain_ref, ...), custom_call_target="tpu_custom_call" | custom-call | flops 1610612736 | bytes 8388608 | tf_op jit(solution)/shard_map/project/pallas_call | solution.py:231
  140.2 5.6 %collective-permute-done.2 = bf16[1,2,512,128]{3,2,1,0:T(8,128)(2,1)S(1)} collective-permute-done((bf16[1,2,512,128]{3,2,1,0:T(8,128)(2,1)}, bf16[1,2,512,128]{3,2,1,0:T(8,128)(2,1)S(1)}, u32[]{:S(2)}, u32[]{:S(2)}) %collective-permute-start.2) | collective-permute-done | bytes 262176 | tf_op jit(solution)/shard_map/ppermute | solution.py:52
  146.7 14.6 %attend.1 = (bf16[2,512,256]{2,1,0:T(8,128)(2,1)}, f32[2,4,512]{2,1,0:T(4,128)}) custom-call(s32[3]{0:T(128)} %pad_add_fusion.place.refs_0_, s32[2]{0:T(128)} %prefix.3, bf16[2,512,256]{2,1,0:T(8,128)(2,1)} %get-tuple-element.44.q_ref, bf16[2,2,512,128]{3,2,1,0:T(8,128)(2,1)} %pad_maximum_fusion.4.kv_ref), custom_call_target="tpu_custom_call" | custom-call | flops 4294967296 | bytes 1048576 | tf_op jit(solution)/shard_map/attend/pallas_call | solution.py:299
  161.4 21.8 %collective-permute-done.3.refs_5_ = bf16[1024,256]{1,0:T(8,128)(2,1)S(1)} collective-permute-done((bf16[1024,256]{1,0:T(8,128)(2,1)}, bf16[1024,256]{1,0:T(8,128)(2,1)S(1)}, u32[]{:S(2)}, u32[]{:S(2)}) %collective-permute-start.3) | collective-permute-done | bytes 524320 | tf_op jit(solution)/shard_map/ppermute | solution.py:63
  187.8 7.8 %collective-permute-done.4.refs_6_ = bf16[1024,256]{1,0:T(8,128)(2,1)} collective-permute-done((bf16[1024,256]{1,0:T(8,128)(2,1)S(1)}, bf16[1024,256]{1,0:T(8,128)(2,1)}, u32[]{:S(2)}, u32[]{:S(2)}) %collective-permute-start.4) | collective-permute-done | bytes 524320 | tf_op jit(solution)/shard_map/ppermute | solution.py:63
  196.2 10.7 %collective-permute-done.5.refs_7_ = bf16[1024,256]{1,0:T(8,128)(2,1)} collective-permute-done((bf16[1024,256]{1,0:T(8,128)(2,1)}, bf16[1024,256]{1,0:T(8,128)(2,1)}, u32[]{:S(2)}, u32[]{:S(2)}) %collective-permute-start.5) | collective-permute-done | bytes 524320 | tf_op jit(solution)/shard_map/ppermute | solution.py:63
  206.9 26.2 %residual_part.1 = (f32[2,512,2048]{2,1,0:T(8,128)}, bf16[2,512,2048]{2,1,0:T(8,128)(2,1)}, f32[2,512,1024]{2,1,0:T(8,128)}) custom-call(s32[3]{0:T(128)} %pad_add_fusion.place.refs_0_, bf16[2,512,2048]{2,1,0:T(8,128)(2,1)} %refs_1_.3, bf16[2,512,2048]{2,1,0:T(8,128)(2,1)} %refs_4_.1, f32[1,2048]{1,0:T(1,128)} %bitcast.114, bf16[1024,256]{1,0:T(8,128)(2,1)} %bitcast.95, ...), custom_call_target="tpu_custom_call" | custom-call | flops 8589934592 | bytes 25165824 | tf_op jit(solution)/shard_map/residual_part/pallas_call | solution.py:434
  233.1 51.6 %ffn.1 = (bf16[2,512,2048]{2,1,0:T(8,128)(2,1)}, bf16[2,512,2048]{2,1,0:T(8,128)(2,1)}, bf16[2,512,256]{2,1,0:T(8,128)(2,1)}, bf16[2,512,256]{2,1,0:T(8,128)(2,1...) custom-call(s32[3]{0:T(128)} %pad_add_fusion.place.refs_0_, ...), custom_call_target="tpu_custom_call" | custom-call | flops 22548578304 | bytes 29360128 | tf_op jit(solution)/shard_map/ffn/pallas_call | solution.py:549
  284.8 19.6 %attend_back.1 = (f32[2,512,256]{2,1,0:T(8,128)}, f32[2,2,512,128]{3,2,1,0:T(8,128)}) custom-call(s32[3]{0:T(128)} %pad_add_fusion.place.refs_0_, s32[2]{0:T(128)} %prefix.3, bf16[2,512,256]{2,1,0:T(8,128)(2,1)} %get-tuple-element.44.q_ref, bf16[2,2,512,128]{3,2,1,0:T(8,128)(2,1)} %pad_maximum_fusion.4.kv_ref, bf16[2,512,256]{2,1,0:T(8,128)(2,1)} %get-tuple-element.55.d_ref, ...), custom_call_target="tpu_custom_call" | custom-call | flops 10737418240 | bytes 2097152 | tf_op jit(solution)/shard_map/attend_back/pallas_call | solution.py:360
  306.4 10.1 %grad_gate_up.1 = (f32[2,2,512,256]{3,2,1,0:T(8,128)}, bf16[2,2,512,256]{3,2,1,0:T(8,128)(2,1)}) custom-call(s32[3]{0:T(128)} %pad_add_fusion.place.refs_0_, bf16[1024,2048]{1,0:T(8,128)(2,1)} %bitcast.88, bf16[1024,256]{1,0:T(8,128)(2,1)} %bitcast.98, bf16[1024,2048]{1,0:T(8,128)(2,1)} %bitcast.89, bf16[1024,256]{1,0:T(8,128)(2,1)} %bitcast.99), custom_call_target="tpu_custom_call" | custom-call | flops 2147483648 | bytes 9437184 | tf_op jit(solution)/shard_map/grad_gate_up/pallas_call | solution.py:763
  316.5 8.8 %grad_down_out.1 = (f32[2,2,256,512]{3,2,1,0:T(8,128)}, bf16[2,2,256,512]{3,2,1,0:T(8,128)(2,1)}) custom-call(s32[3]{0:T(128)} %pad_add_fusion.place.refs_0_, bf16[1024,256]{1,0:T(8,128)(2,1)} %bitcast.97, bf16[1024,2048]{1,0:T(8,128)(2,1)} %bitcast.90, bf16[1024,256]{1,0:T(8,128)(2,1)} %bitcast.96, bf16[1024,2048]{1,0:T(8,128)(2,1)} %bitcast.91), custom_call_target="tpu_custom_call" | custom-call | flops 2147483648 | bytes 9437184 | tf_op jit(solution)/shard_map/grad_down_out/pallas_call | solution.py:763
  326.6 8.9 %head_back.1 = (bf16[2,512,384]{2,1,0:T(8,128)(2,1)}, f32[1,384]{1,0:T(1,128)}) custom-call(f32[2,512,384]{2,1,0:T(8,128)} %get-tuple-element.54.raw_ref, f32[2,512,256]{2,1,0:T(8,128)} %get-tuple-element.57.dq_ref, f32[2,512,128]{2,1,0:T(8,128)} %add_bitcast_fusion.1.dkv_ref, f32[1,384]{1,0:T(1,128)} %concatenate.26.hgain_ref, ...), custom_call_target="tpu_custom_call" | custom-call | flops 1207959552 | bytes 5505024 | tf_op jit(solution)/shard_map/head_back/pallas_call | solution.py:621
  335.6 7.2 %grad_qkv.1 = (f32[2,1,512,384]{3,2,1,0:T(8,128)}, bf16[2,1,512,384]{3,2,1,0:T(8,128)(2,1)}) custom-call(s32[3]{0:T(128)} %pad_add_fusion.place.refs_0_, bf16[1024,2048]{1,0:T(8,128)(2,1)} %bitcast.120, bf16[1024,384]{1,0:T(8,128)(2,1)} %bitcast.122), custom_call_target="tpu_custom_call" | custom-call | flops 1610612736 | bytes 4980736 | tf_op jit(solution)/shard_map/grad_qkv/pallas_call | solution.py:763
  343.0 16.1 %psum.7 = bf16[1,128]{1,0:T(2,128)(2,1)S(1)} all-reduce(f32[1,128]{1,0:T(1,128)S(1)} %maximum_bitcast_fusion), channel_id=1, replica_groups=mesh['fsdp'=4,'ctx'=2,'tp'=4] {'tp'}, use_global_device_ids=true, to_apply=%region_1.0 | all-reduce | flops 128 | bytes 768 | tf_op jit(solution)/shard_map/psum | solution.py:890
  367.8 16.2 %collective-permute-done.28 = bf16[1,512,384]{2,1,0:T(8,128)(2,1)S(1)} collective-permute-done((bf16[1,512,384]{2,1,0:T(8,128)(2,1)S(1)}, bf16[1,512,384]{2,1,0:T(8,128)(2,1)S(1)}, u32[]{:S(2)}, u32[]{:S(2)}) %collective-permute-start.28) | collective-permute-done | bytes 393248 | tf_op jit(solution)/shard_map/ppermute | solution.py:52
  398.8 8.2 %collective-permute-done.35 = bf16[2,512,256]{2,1,0:T(8,128)(2,1)S(1)} collective-permute-done((bf16[2,512,256]{2,1,0:T(8,128)(2,1)S(1)}, bf16[2,512,256]{2,1,0:T(8,128)(2,1)S(1)}, u32[]{:S(2)}, u32[]{:S(2)}) %collective-permute-start.35) | collective-permute-done | bytes 524320 | tf_op jit(solution)/shard_map/ppermute | solution.py:52
  407.2 25.7 %input_part.1 = (bf16[2,512,2048]{2,1,0:T(8,128)(2,1)}, f32[1,2048]{1,0:T(1,128)}) custom-call(s32[3]{0:T(128)} %pad_add_fusion.place.refs_0_, bf16[2,512,2048]{2,1,0:T(8,128)(2,1)} %refs_1_.3, bf16[2,512,2048]{2,1,0:T(8,128)(2,1)} %get-tuple-element.53.refs_2_, f32[1,2048]{1,0:T(1,128)} %bitcast.113, bf16[1024,384]{1,0:T(8,128)(2,1)} %bitcast.123, ...), custom_call_target="tpu_custom_call" | custom-call | flops 6442450944 | bytes 12582912 | tf_op jit(solution)/shard_map/input_part/pallas_call | solution.py:707
  (180 shorter events, 83.2 us)
Async XLA Ops:
  7.2 96.3 %all-gather.6.cloned.1.call-start = ((), (), s32[]{:S(2)}) async-start(), calls=%async_computation | async-start | bytes 8912896 | tf_op jit(solution)/shard_map/all_gather | solution.py:830
  9.2 397.9 %all-gather.8.cloned.1.call-start = ((), (), s32[]{:S(2)}) async-start(), calls=%async_computation.1 | async-start | bytes 6684672 | tf_op jit(solution)/shard_map/all_gather | solution.py:842
  71.3 37.8 %collective-permute-start.1 = (bf16[2,512,384]{2,1,0:T(8,128)(2,1)}, bf16[2,512,384]{2,1,0:T(8,128)(2,1)}, u32[]{:S(2)}, u32[]{:S(2)}) collective-permute-start(bf16[2,512,384]{2,1,0:T(8,128)(2,1)} %pad_maximum_fusion.3), channel_id=1, source_target_pairs={{0,8},{8,0},{16,24},{24,16},{1,9},{9,1},{17,25},{25,17},{2,10},{10... | collective-permute-start | bytes 2359304 | tf_op jit(solution)/shard_map/ppermute | solution.py:52
  80.4 28.7 %collective-permute-start.14 = (bf16[2,128,512]{2,1,0:T(8,128)(2,1)S(1)}, bf16[2,128,512]{2,1,0:T(8,128)(2,1)S(1)}, u32[]{:S(2)}, u32[]{:S(2)}) collective-permute-start(bf16[2,128,512]{2,1,0:T(8,128)(2,1)S(1)} %get-tuple-element.110), channel_id=1, source_target_pairs={{0,1},{1,2},{2,3},{3,0},{4,5},{5,6},{6,7},{7,4},{8,9},{9,10},{10,1... | collective-permute-start | bytes 786440 | tf_op jit(solution)/shard_map/ppermute | solution.py:63
  122.1 16.4 %collective-permute-start.16 = (bf16[2,128,512]{2,1,0:T(8,128)(2,1)S(1)}, bf16[2,128,512]{2,1,0:T(8,128)(2,1)S(1)}, u32[]{:S(2)}, u32[]{:S(2)}) collective-permute-start(bf16[2,128,512]{2,1,0:T(8,128)(2,1)S(1)} %collective-permute-done.15), channel_id=1, source_target_pairs={{0,1},{1,2},{2,3},{3,0},{4,5},{5,6},{6,7},{7,4},{8,9},{9,10},{10,1... | collective-permute-start | bytes 786440 | tf_op jit(solution)/shard_map/ppermute | solution.py:63
  138.0 45.4 %collective-permute-start.10 = (bf16[4,2,128,512]{3,2,1,0:T(8,128)(2,1)S(1)}, bf16[4,2,128,512]{3,2,1,0:T(8,128)(2,1)}, u32[]{:S(2)}, u32[]{:S(2)}) collective-permute-start(bf16[4,2,128,512]{3,2,1,0:T(8,128)(2,1)S(1)} %pad_maximum_fusion.1.refs_8_.refs_11_), channel_id=1, source_target_pairs={{0,4},{4,0},{1,5},{5,1},{2,6},{6,2},{3,7},{7,3},{8,12},{12,8},{9,1... | collective-permute-start | bytes 3145736 | tf_op jit(solution)/shard_map/ppermute | solution.py:52
  138.6 49.2 %collective-permute-start.17 = (bf16[4,2,128,512]{3,2,1,0:T(8,128)(2,1)S(1)}, bf16[4,2,128,512]{3,2,1,0:T(8,128)(2,1)}, u32[]{:S(2)}, u32[]{:S(2)}) collective-permute-start(bf16[4,2,128,512]{3,2,1,0:T(8,128)(2,1)S(1)} %pad_maximum_fusion.2.refs_12_.refs_7_), channel_id=1, source_target_pairs={{0,4},{4,0},{1,5},{5,1},{2,6},{6,2},{3,7},{7,3},{8,12},{12,8},{9,1... | collective-permute-start | bytes 3145736 | tf_op jit(solution)/shard_map/ppermute | solution.py:52
  161.3 22.0 %collective-permute-start.3 = (bf16[1024,256]{1,0:T(8,128)(2,1)}, bf16[1024,256]{1,0:T(8,128)(2,1)S(1)}, u32[]{:S(2)}, u32[]{:S(2)}) collective-permute-start(bf16[1024,256]{1,0:T(8,128)(2,1)} %bitcast.94), channel_id=1, source_target_pairs={{0,1},{1,2},{2,3},{3,0},{4,5},{5,6},{6,7},{7,4},{8,9},{9,10},{10,1... | collective-permute-start | bytes 1572872 | tf_op jit(solution)/shard_map/ppermute | solution.py:63
  161.4 34.8 %collective-permute-start.11 = (bf16[4,2,128,512]{3,2,1,0:T(8,128)(2,1)S(1)}, bf16[4,2,128,512]{3,2,1,0:T(8,128)(2,1)}, u32[]{:S(2)}, u32[]{:S(2)}) collective-permute-start(bf16[4,2,128,512]{3,2,1,0:T(8,128)(2,1)S(1)} %pad_maximum_fusion.1.refs_8_.refs_11_), channel_id=1, source_target_pairs={{0,8},{8,0},{16,24},{24,16},{1,9},{9,1},{17,25},{25,17},{2,10},{10... | collective-permute-start | bytes 3145736 | tf_op jit(solution)/shard_map/ppermute | solution.py:52
  183.3 23.7 %collective-permute-start.18 = (bf16[4,2,128,512]{3,2,1,0:T(8,128)(2,1)S(1)}, bf16[4,2,128,512]{3,2,1,0:T(8,128)(2,1)}, u32[]{:S(2)}, u32[]{:S(2)}) collective-permute-start(bf16[4,2,128,512]{3,2,1,0:T(8,128)(2,1)S(1)} %pad_maximum_fusion.2.refs_12_.refs_7_), channel_id=1, source_target_pairs={{0,8},{8,0},{16,24},{24,16},{1,9},{9,1},{17,25},{25,17},{2,10},{10... | collective-permute-start | bytes 3145736 | tf_op jit(solution)/shard_map/ppermute | solution.py:52
  183.4 23.6 %collective-permute-start.12 = (bf16[4,2,128,512]{3,2,1,0:T(8,128)(2,1)}, bf16[4,2,128,512]{3,2,1,0:T(8,128)(2,1)}, u32[]{:S(2)}, u32[]{:S(2)}) collective-permute-start(bf16[4,2,128,512]{3,2,1,0:T(8,128)(2,1)} %collective-permute-done.10.refs_9_.refs_12_), channel_id=1, source_target_pairs={{0,8},{8,0},{16,24},{24,16},{1,9},{9,1},{17,25},{25,17},{2,10},{10... | collective-permute-start | bytes 3145736 | tf_op jit(solution)/shard_map/ppermute | solution.py:52
  187.8 19.1 %collective-permute-start.19 = (bf16[4,2,128,512]{3,2,1,0:T(8,128)(2,1)}, bf16[4,2,128,512]{3,2,1,0:T(8,128)(2,1)}, u32[]{:S(2)}, u32[]{:S(2)}) collective-permute-start(bf16[4,2,128,512]{3,2,1,0:T(8,128)(2,1)} %collective-permute-done.17.refs_13_.refs_8_), channel_id=1, source_target_pairs={{0,8},{8,0},{16,24},{24,16},{1,9},{9,1},{17,25},{25,17},{2,10},{10... | collective-permute-start | bytes 3145736 | tf_op jit(solution)/shard_map/ppermute | solution.py:52
  305.4 20.4 %collective-permute-start.20 = (bf16[1,2,512,128]{3,2,1,0:T(8,128)(2,1)S(1)}, bf16[1,2,512,128]{3,2,1,0:T(8,128)(2,1)S(1)}, u32[]{:S(2)}, u32[]{:S(2)}) collective-permute-start(bf16[1,2,512,128]{3,2,1,0:T(8,128)(2,1)S(1)} %slice.175), channel_id=1, source_target_pairs={{0,4},{4,0},{1,5},{5,1},{2,6},{6,2},{3,7},{7,3},{8,12},{12,8},{9,1... | collective-permute-start | bytes 786440 | tf_op jit(solution)/shard_map/ppermute | solution.py:52
  316.5 42.6 %collective-permute-start.33 = (bf16[2,2,512,256]{3,2,1,0:T(8,128)(2,1)}, bf16[2,2,512,256]{3,2,1,0:T(8,128)(2,1)}, u32[]{:S(2)}, u32[]{:S(2)}) collective-permute-start(bf16[2,2,512,256]{3,2,1,0:T(8,128)(2,1)} %get-tuple-element.74), channel_id=1, source_target_pairs={{0,8},{8,0},{16,24},{24,16},{1,9},{9,1},{17,25},{25,17},{2,10},{10... | collective-permute-start | bytes 3145736 | tf_op jit(solution)/shard_map/ppermute | solution.py:52
  325.3 41.0 %collective-permute-start.30 = (bf16[2,2,256,512]{3,2,1,0:T(8,128)(2,1)}, bf16[2,2,256,512]{3,2,1,0:T(8,128)(2,1)S(1)}, u32[]{:S(2)}, u32[]{:S(2)}) collective-permute-start(bf16[2,2,256,512]{3,2,1,0:T(8,128)(2,1)} %get-tuple-element.70), channel_id=1, source_target_pairs={{0,8},{8,0},{16,24},{24,16},{1,9},{9,1},{17,25},{25,17},{2,10},{10... | collective-permute-start | bytes 3145736 | tf_op jit(solution)/shard_map/ppermute | solution.py:52
  335.5 28.9 %collective-permute-start.21 = (bf16[1024,384]{1,0:T(8,128)(2,1)}, bf16[1024,384]{1,0:T(8,128)(2,1)}, u32[]{:S(2)}, u32[]{:S(2)}) collective-permute-start(bf16[1024,384]{1,0:T(8,128)(2,1)} %bitcast.121), channel_id=1, source_target_pairs={{0,1},{1,2},{2,3},{3,0},{4,5},{5,6},{6,7},{7,4},{8,9},{9,10},{10,1... | collective-permute-start | bytes 2359304 | tf_op jit(solution)/shard_map/ppermute | solution.py:63
  342.8 19.0 %collective-permute-start.27 = (bf16[2,1,512,384]{3,2,1,0:T(8,128)(2,1)}, bf16[2,1,512,384]{3,2,1,0:T(8,128)(2,1)}, u32[]{:S(2)}, u32[]{:S(2)}) collective-permute-start(bf16[2,1,512,384]{3,2,1,0:T(8,128)(2,1)} %get-tuple-element.67), channel_id=1, source_target_pairs={{0,8},{8,0},{16,24},{24,16},{1,9},{9,1},{17,25},{25,17},{2,10},{10... | collective-permute-start | bytes 2359304 | tf_op jit(solution)/shard_map/ppermute | solution.py:52
  360.7 24.5 %collective-permute-start.34 = (bf16[2,512,256]{2,1,0:T(8,128)(2,1)S(1)}, bf16[2,512,256]{2,1,0:T(8,128)(2,1)S(1)}, u32[]{:S(2)}, u32[]{:S(2)}) collective-permute-start(bf16[2,512,256]{2,1,0:T(8,128)(2,1)S(1)} %fusion.7), channel_id=1, source_target_pairs={{0,16},{8,24},{16,0},{24,8},{1,17},{9,25},{17,1},{25,9},{2,18},{10... | collective-permute-start | bytes 1572872 | tf_op jit(solution)/shard_map/ppermute | solution.py:52
  363.3 20.7 %collective-permute-start.28 = (bf16[1,512,384]{2,1,0:T(8,128)(2,1)S(1)}, bf16[1,512,384]{2,1,0:T(8,128)(2,1)S(1)}, u32[]{:S(2)}, u32[]{:S(2)}) collective-permute-start(bf16[1,512,384]{2,1,0:T(8,128)(2,1)S(1)} %fusion.8), channel_id=1, source_target_pairs={{0,16},{8,24},{16,0},{24,8},{1,17},{9,25},{17,1},{25,9},{2,18},{10... | collective-permute-start | bytes 1179656 | tf_op jit(solution)/shard_map/ppermute | solution.py:52
  364.4 22.0 %collective-permute-start.22 = (bf16[1024,384]{1,0:T(8,128)(2,1)}, bf16[1024,384]{1,0:T(8,128)(2,1)}, u32[]{:S(2)}, u32[]{:S(2)}) collective-permute-start(bf16[1024,384]{1,0:T(8,128)(2,1)} %collective-permute-done.21.refs_5_), channel_id=1, source_target_pairs={{0,1},{1,2},{2,3},{3,0},{4,5},{5,6},{6,7},{7,4},{8,9},{9,10},{10,1... | collective-permute-start | bytes 2359304 | tf_op jit(solution)/shard_map/ppermute | solution.py:63
  366.7 25.9 %collective-permute-start.31 = (bf16[2,256,512]{2,1,0:T(8,128)(2,1)S(1)}, bf16[2,256,512]{2,1,0:T(8,128)(2,1)S(1)}, u32[]{:S(2)}, u32[]{:S(2)}) collective-permute-start(bf16[2,256,512]{2,1,0:T(8,128)(2,1)S(1)} %fusion.6), channel_id=1, source_target_pairs={{0,16},{8,24},{16,0},{24,8},{1,17},{9,25},{17,1},{25,9},{2,18},{10... | collective-permute-start | bytes 1572872 | tf_op jit(solution)/shard_map/ppermute | solution.py:52
  385.4 21.6 %collective-permute-start.35 = (bf16[2,512,256]{2,1,0:T(8,128)(2,1)S(1)}, bf16[2,512,256]{2,1,0:T(8,128)(2,1)S(1)}, u32[]{:S(2)}, u32[]{:S(2)}) collective-permute-start(bf16[2,512,256]{2,1,0:T(8,128)(2,1)S(1)} %fusion.1), channel_id=1, source_target_pairs={{0,4},{4,0},{1,5},{5,1},{2,6},{6,2},{3,7},{7,3},{8,12},{12,8},{9,1... | collective-permute-start | bytes 1572872 | tf_op jit(solution)/shard_map/ppermute | solution.py:52
  386.4 20.7 %collective-permute-start.23 = (bf16[1024,384]{1,0:T(8,128)(2,1)}, bf16[1024,384]{1,0:T(8,128)(2,1)}, u32[]{:S(2)}, u32[]{:S(2)}) collective-permute-start(bf16[1024,384]{1,0:T(8,128)(2,1)} %collective-permute-done.22.refs_6_), channel_id=1, source_target_pairs={{0,1},{1,2},{2,3},{3,0},{4,5},{5,6},{6,7},{7,4},{8,9},{9,10},{10,1... | collective-permute-start | bytes 2359304 | tf_op jit(solution)/shard_map/ppermute | solution.py:63
  392.8 40.9 %collective-permute-start.32 = (bf16[2,256,512]{2,1,0:T(8,128)(2,1)S(1)}, bf16[2,256,512]{2,1,0:T(8,128)(2,1)S(1)}, u32[]{:S(2)}, u32[]{:S(2)}) collective-permute-start(bf16[2,256,512]{2,1,0:T(8,128)(2,1)S(1)} %fusion.3), channel_id=1, source_target_pairs={{0,4},{4,0},{1,5},{5,1},{2,6},{6,2},{3,7},{7,3},{8,12},{12,8},{9,1... | collective-permute-start | bytes 1572872 | tf_op jit(solution)/shard_map/ppermute | solution.py:52
  (35 other events, 745.1 us)
Sparse Core Ops, SparseCore 0:
  10.8 92.6 all-gather.5
  105.8 76.0 all-gather.7
